TPU v7x, 32 devices: a whole 2x2x4 slice. The times are simulated.
32 devices in a mesh: space: 8 (over z, y), chan: 4 (over x, core).
Axes of the slice: x: 2, y: 2, z: 4, core: 2. Of those that a mesh axis runs over, the one named last changes fastest.
Arguments:
- features: bfloat16 [128, 64, 128], P('space'), may hold values from -6 to 6
- neighbours: int32 [128, 26], P('space'), may hold values from -1 to 127, as said below
- parent_index: int32 [128], P('space'), may hold values from 0 to 31, as said below
- octant: int32 [128], P('space'), may hold values from 0 to 7, as said below
- parent_dest: int32 [32], P('space'), may hold values from 0 to 63, as said below
- conv_fine: bfloat16 [128, 3456], P('chan'), may hold values from -0.109375 to 0.109375
- conv_down: bfloat16 [256, 3456], P('chan'), may hold values from -0.15625 to 0.15625
- conv_coarse: bfloat16 [256, 6912], P('chan'), may hold values from -0.15625 to 0.15625
- norm_gain: float32 [256], P('chan'), may hold values from 0.25 to 1.75
Outputs:
- coarse_parents: bfloat16 [256, 4096], P('chan', 'space')
Inputs may be any that keep to these rules, and one draw needn't show every extreme that they name: Brick n lies on device n // 16 of space. Device d holds 16 distinct positions of a slab of 2 x 4 x 4 brick positions (x = 2 d or 2 d + 1, y, z); brick n's position gives parent_index[n] = d * 4 + (y // 2) * 2 + z // 2 and octant[n] = x % 2 + 2 (y % 2) + 4 (z % 2). neighbours[n, k] is the brick at the k-th offset (a, b, c), a, b, c in -1, 0, 1, (0, 0, 0) left out, in increasing 9 a + 3 b + c, or -1 where that position holds no brick. `parent_index`: as stated for neighbours. `octant`: as stated for neighbours. parent_dest[g] = owner * 8 + slot, where the owner of a parent of device d is d - 1, d or d + 1. At most 2 parents of one device go to each of its two neighbours, and some device sends 2 to a neighbour; some owner receives 8 parents. An owner's slots are filled from 0 upward without gaps, in order of source device and then of parent.
All inputs are finite; a program needn't handle non-finite values.
Results may differ from a plain program's by a relative error of at most 0.0065.
Values may be sent and summed in bfloat16 or wider, within the bound.
A program may use at most 64 MiB of HBM per device.

v0:
```python
import functools

import jax
import jax.numpy as jnp
import numpy as np
from jax import lax
from jax.experimental import pallas as pl
from jax.experimental.pallas import tpu as pltpu
from jax.sharding import PartitionSpec as P

EDGE = 4
SLAB_Y = 4
SLAB_Z = 4
NY = SLAB_Y * EDGE
NZ = SLAB_Z * EDGE
LAYER = NY * NZ
NX = 2 * EDGE
CY = NY // 2
CZ = NZ // 2
CLAYER = CY * CZ
CX = NX // 2
FACE = EDGE * EDGE
epsilon = 1e-06
BF = jnp.bfloat16
F32 = jnp.float32
NT = (((1,), (1,)), ((), ()))


def iota(shape, dim):
    return lax.broadcasted_iota(jnp.int32, shape, dim)


def one(cond):
    return jnp.where(cond, 1.0, 0.0).astype(BF)


def pick(a, b):
    return jnp.dot(a, b, preferred_element_type=F32)


def tables(n_chan, fine, coarse_own):
    def held(cond):
        return jnp.asarray(np.asarray(cond, np.float32).astype(jnp.bfloat16))

    def grid(rows, columns):
        return np.arange(rows)[:, None], np.arange(columns)[None, :]

    wide = fine // n_chan
    coarse = coarse_own * n_chan
    r, q = grid(n_chan * fine, n_chan * fine)
    perm_h = held((r % fine) // wide * fine + r // fine * wide + r % wide == q)
    perm_c = held((r % fine) // coarse_own * coarse + r // fine * coarse_own + r % coarse_own == q)
    r, q = grid(9 * CLAYER, LAYER)
    bc, at = r // CLAYER, r % CLAYER
    y = 2 * (at // CZ) + bc // 3 - 1
    z = 2 * (at % CZ) + bc % 3 - 1
    sel_d = held((y >= 0) & (z >= 0) & (y * NZ + z == q))
    r, q = grid(9 * CLAYER, CLAYER)
    bc, at = r // CLAYER, r % CLAYER
    par, yz = at // FACE, at % FACE
    y = par // (SLAB_Z // 2) * EDGE + yz // EDGE + bc // 3 - 1
    z = par % (SLAB_Z // 2) * EDGE + yz % EDGE + bc % 3 - 1
    sel_c = held((y >= 0) & (z >= 0) & (z < CZ) & (y * CZ + z == q))
    return perm_h, perm_c, sel_d, sel_c


def fused_kernel(
    n_space, n_chan, bricks, slots,
    feat_hbm, parent_hbm, octant_hbm, dest_hbm, wf_hbm, wd_hbm, wc_hbm, gain_hbm,
    perm_h_hbm, perm_c_hbm, sel_d_hbm, sel_c_hbm,
    out,
    feat, wf, gain, parent_in, octant_in, dest_in, meta, wd, wc, fh, mh, s_buf, mask, g_buf,
    perm_h, perm_c, sel_d, sel_c, d_buf, c_buf, e_buf, pb, pw, ohd,
    wsem, s1, r1, s2, r2, hs2, hr2, s3, r3, hs3, hr3, s4, r4, ws4, wr4,
):
    sp = lax.axis_index("space")
    me = lax.axis_index("chan")
    has_prev = sp > 0
    has_next = sp < n_space - 1
    fine = feat.shape[2]
    wide = fine // n_chan
    parents = dest_in.shape[1]
    cells = EDGE**3
    coarse_own = wd.shape[0]
    coarse = coarse_own * n_chan
    taps2 = 9
    half = fine // coarse_own
    crows = CLAYER // half
    rows = LAYER // n_chan

    def rc(src, dst, ss, rs, space, chan):
        return pltpu.make_async_remote_copy(
            src_ref=src,
            dst_ref=dst,
            send_sem=ss,
            recv_sem=rs,
            device_id={"space": space, "chan": chan},
            device_id_type=pl.DeviceIdType.MESH,
        )

    peers = [lax.rem(me + k, n_chan) for k in range(1, n_chan)]
    barrier = pltpu.get_barrier_semaphore()

    def greet(space, chan):
        pl.semaphore_signal(
            barrier,
            inc=1,
            device_id={"space": space, "chan": chan},
            device_id_type=pl.DeviceIdType.MESH,
        )

    @pl.when(has_prev)
    def _():
        for chan in range(n_chan):
            greet(sp - 1, chan)

    @pl.when(has_next)
    def _():
        for chan in range(n_chan):
            greet(sp + 1, chan)

    for chan in peers:
        greet(sp, chan)

    loads = [
        pltpu.make_async_copy(src, dst, wsem.at[k])
        for k, (src, dst) in enumerate(
            (
                (parent_hbm, parent_in),
                (octant_hbm, octant_in),
                (dest_hbm, dest_in),
                (feat_hbm, feat),
                (wf_hbm, wf),
                (gain_hbm, gain),
                (perm_h_hbm, perm_h),
                (sel_d_hbm, sel_d),
                (wd_hbm, wd),
                (perm_c_hbm, perm_c),
                (sel_c_hbm, sel_c),
                (wc_hbm, wc),
            )
        )
    ]
    for load in loads:
        load.start()

    @pl.when(jnp.logical_not(has_prev))
    def _():
        fh[0] = jnp.zeros(fh.shape[1:], BF)
        mh[0] = jnp.zeros(mh.shape[1:], jnp.int32)
        g_buf[0] = jnp.zeros(g_buf.shape[1:], BF)
        c_buf[0] = jnp.zeros(c_buf.shape[1:], BF)
        pb[0] = jnp.zeros(pb.shape[1:], BF)
        pw[0] = jnp.zeros(pw.shape[1:], F32)

    @pl.when(jnp.logical_not(has_next))
    def _():
        fh[1] = jnp.zeros(fh.shape[1:], BF)
        mh[1] = jnp.zeros(mh.shape[1:], jnp.int32)
        c_buf[CX + 1] = jnp.zeros(c_buf.shape[1:], BF)
        pb[2] = jnp.zeros(pb.shape[1:], BF)
        pw[2] = jnp.zeros(pw.shape[1:], F32)

    blank_y = jnp.zeros((NX + 2, NZ, 3 * fine), BF)
    s_buf[:, 0:NZ, :] = blank_y
    s_buf[:, NZ + LAYER : 2 * NZ + LAYER, :] = blank_y

    lanes = meta.shape[1]
    columns = bricks * FACE
    spread = jnp.where(iota((lanes, columns), 1) // FACE == iota((lanes, columns), 0), 1.0, 0.0)
    face = iota((1, columns), 1) % FACE
    row_ids = iota((LAYER, columns), 0)

    meta[...] = jnp.zeros(meta.shape, jnp.int32)
    for load in loads[:4]:
        load.wait()
    local = parent_in[...] - sp * parents
    octant = octant_in[...]
    y_pos = 2 * (local // (SLAB_Z // 2)) + octant // 2 % 2
    z_pos = 2 * (local % (SLAB_Z // 2)) + octant // 4
    meta[0:1, 0:bricks] = octant % 2 + 2 * y_pos + 2 * SLAB_Y * z_pos
    meta[1:2, 0:parents] = dest_in[...] - (sp - 1) * slots

    def keys_of(meta_block):
        code = jnp.dot(meta_block.astype(F32), spread, preferred_element_type=F32)[0:1].astype(jnp.int32)
        x_bit = code % 2
        y_pos = code // 2 % SLAB_Y
        z_pos = code // (2 * SLAB_Y)
        y = y_pos * EDGE + face // EDGE
        z = z_pos * EDGE + face % EDGE
        return x_bit, y, z

    def one_hot(key, x_want, c):
        x_bit, y, z = key
        fits = (x_bit == x_want) & (z - c >= 0) & (z - c < NZ)
        return one(row_ids == jnp.where(fits, y * NZ + z - c, -1))

    faces = jnp.concatenate(
        [feat[:, i * FACE : (i + 1) * FACE, :].reshape(columns, fine) for i in range(EDGE)], axis=1
    )
    key = keys_of(meta[...])
    for x in range(2):
        for c in (-1, 0, 1):
            hot = one_hot(key, x, c)
            placed = pick(hot, faces).astype(BF)
            for i in range(EDGE):
                s_buf[1 + EDGE * x + i, NZ : NZ + LAYER, (c + 1) * fine : (c + 2) * fine] = placed[
                    :, i * fine : (i + 1) * fine
                ]
            if c == 0:
                mask[x] = pick(hot, jnp.ones((columns, fine), BF))

    def hidden_layer(x):
        parts = []
        for a in (-1, 0, 1):
            for b in (-1, 0, 1):
                parts.append(s_buf[x + 1 + a, (1 + b) * NZ : (1 + b) * NZ + LAYER, :])
        total = lax.dot_general(jnp.concatenate(parts, axis=1), wf[...], NT, preferred_element_type=F32)
        total = jnp.where(mask[x // EDGE][:, 0:wide] > 0.5, jnp.maximum(total, 0.0), 0.0)
        packed = jnp.concatenate([total[j * rows : (j + 1) * rows] for j in range(n_chan)], axis=1)
        g_buf[x + 1, me] = packed.astype(BF)

    def send_layer(x):
        for k, chan in enumerate(peers):
            rc(g_buf.at[x + 1, me], g_buf.at[x + 1, me], s2.at[x, k], r2.at[x, me], sp, chan).start()

    early = NX // 2
    for load in loads[4:6]:
        load.wait()
    for x in range(1, early):
        hidden_layer(x)

    pl.semaphore_wait(
        barrier, n_chan - 1 + n_chan * (has_prev.astype(jnp.int32) + has_next.astype(jnp.int32))
    )

    up_feat = rc(feat.at[:, pl.ds((EDGE - 1) * FACE, FACE), :], fh.at[0], s1.at[0, 0], r1.at[0, 0], sp + 1, me)
    up_meta = rc(meta, mh.at[0], s1.at[0, 1], r1.at[0, 1], sp + 1, me)
    dn_feat = rc(feat.at[:, pl.ds(0, FACE), :], fh.at[1], s1.at[1, 0], r1.at[1, 0], sp - 1, me)
    dn_meta = rc(meta, mh.at[1], s1.at[1, 1], r1.at[1, 1], sp - 1, me)

    @pl.when(has_next)
    def _():
        up_meta.start()
        up_feat.start()

    @pl.when(has_prev)
    def _():
        dn_meta.start()
        dn_feat.start()

    for x in range(1, early):
        send_layer(x)
    for x in range(early, NX - 1):
        hidden_layer(x)
        send_layer(x)

    lane_par = jnp.where(
        iota((lanes, parents * cells), 1) // cells == iota((lanes, parents * cells), 0), 1.0, 0.0
    )

    def dest_table(k):
        block = meta[...] if k == 1 else mh[k // 2]
        rel = jnp.dot(block.astype(F32), lane_par, preferred_element_type=F32)[1:2].astype(jnp.int32)
        slot = rel - (2 - k) * slots
        target = slot * cells + iota((1, parents * cells), 1) % cells
        ids = iota((slots * cells, parents * cells), 0)
        ohd[k] = one(ids == jnp.where((slot >= 0) & (slot < slots), target, -1))

    dest_table(1)

    def halo_layer(side):
        k = keys_of(mh[side])
        block = fh[side].reshape(columns, fine)
        for c in (-1, 0, 1):
            s_buf[0 if side == 0 else NX + 1, NZ : NZ + LAYER, (c + 1) * fine : (c + 2) * fine] = pick(
                one_hot(k, 1 - side, c), block
            ).astype(BF)

    @pl.when(has_next)
    def _():
        dn_meta.wait_recv()
        dn_feat.wait_recv()

    halo_layer(1)
    hidden_layer(NX - 1)

    @pl.when(has_next)
    def _():
        for chan in range(n_chan):
            rc(g_buf.at[NX, me], g_buf.at[0, me], hs2.at[chan], hr2.at[me], sp + 1, chan).start()

    send_layer(NX - 1)

    @pl.when(has_prev)
    def _():
        up_meta.wait_recv()
        up_feat.wait_recv()

    halo_layer(0)
    hidden_layer(0)
    send_layer(0)

    def wait_layer(x):
        for k in range(1, n_chan):
            src = lax.rem(me + k, n_chan)
            rc(g_buf.at[x + 1, src], g_buf.at[x + 1, src], s2.at[x, 0], r2.at[x, src], sp, src).wait_recv()

    def spread_layers(buf, at, perm, height, width, parts):
        gathered = jnp.concatenate(
            [jnp.concatenate([buf[x, s] for s in range(n_chan)], axis=1) for x in at], axis=0
        )
        moved = pick(gathered, perm[...]).astype(BF)
        layers = [
            jnp.concatenate(
                [moved[i * height : (i + 1) * height, j * width : (j + 1) * width] for j in range(parts)],
                axis=0,
            )
            for i in range(len(at))
        ]
        return jnp.concatenate(layers, axis=1)

    def fill_d(at):
        filled = pick(sel_d[...], spread_layers(g_buf, at, perm_h, rows, fine, n_chan)).astype(BF)
        for i, x in enumerate(at):
            d_buf[:, x * fine : (x + 1) * fine] = filled[:, i * fine : (i + 1) * fine]

    def down(at):
        stacked = []
        for x in at:
            stacked.append(
                jnp.concatenate(
                    [
                        d_buf[bc * CLAYER : (bc + 1) * CLAYER, (2 * x + a) * fine : (2 * x + a + 1) * fine]
                        for a in range(3)
                        for bc in range(taps2)
                    ],
                    axis=1,
                )
            )
        pieces = lax.dot_general(jnp.concatenate(stacked, axis=0), wd[...], NT, preferred_element_type=F32)
        for i, x in enumerate(at):
            live = pick(sel_d[4 * CLAYER : 5 * CLAYER, :], mask[x // 2].astype(BF))[:, 0:coarse_own]
            part = pieces[i * CLAYER : (i + 1) * CLAYER]
            part = jnp.where(live > 0.5, jnp.maximum(part, 0.0), 0.0)
            c_buf[x + 1, me] = jnp.concatenate(
                [part[j * crows : (j + 1) * crows] for j in range(half)], axis=1
            ).astype(BF)

    inner = list(range(1, CX - 1))
    for load in loads[6:9]:
        load.wait()
    for x in range(1, NX - 1):
        wait_layer(x)
    fill_d(list(range(2, NX)))
    down(inner)

    @pl.when(has_prev)
    def _():
        for chan in range(n_chan):
            rc(g_buf.at[0, chan], g_buf.at[0, chan], hs2.at[chan], hr2.at[chan], sp - 1, chan).wait_recv()

    wait_layer(NX - 1)
    wait_layer(0)
    fill_d([0, 1, NX])
    down([0, CX - 1])

    @pl.when(has_next)
    def _():
        for chan in range(n_chan):
            rc(c_buf.at[CX, me], c_buf.at[0, me], hs3.at[0, chan], hr3.at[0, me], sp + 1, chan).start()

    @pl.when(has_prev)
    def _():
        for chan in range(n_chan):
            rc(c_buf.at[1, me], c_buf.at[CX + 1, me], hs3.at[1, chan], hr3.at[1, me], sp - 1, chan).start()

    own_c = c_buf.at[pl.ds(1, CX), me]
    for k, chan in enumerate(peers):
        rc(own_c, own_c, s3.at[k], r3.at[me], sp, chan).start()

    dest_table(0)
    dest_table(2)
    for load in loads[9:]:
        load.wait()

    for k in range(1, n_chan):
        src = lax.rem(me + k, n_chan)
        ref = c_buf.at[pl.ds(1, CX), src]
        rc(ref, ref, s3.at[0], r3.at[src], sp, src).wait_recv()

    def fill_e(at):
        filled = pick(sel_c[...], spread_layers(c_buf, at, perm_c, crows, coarse, half)).astype(BF)
        for i, x in enumerate(at):
            e_buf[:, x * coarse : (x + 1) * coarse] = filled[:, i * coarse : (i + 1) * coarse]

    def coarse_taps(a, total):
        for bc in range(taps2):
            block = jnp.concatenate(
                [
                    e_buf[
                        bc * CLAYER + g * FACE : bc * CLAYER + (g + 1) * FACE,
                        (x + a) * coarse : (x + a + 1) * coarse,
                    ]
                    for g in range(parents)
                    for x in range(CX)
                ],
                axis=0,
            )
            t = a * taps2 + bc
            term = lax.dot_general(wc[:, t * coarse : (t + 1) * coarse], block, NT, preferred_element_type=F32)
            total = term if total is None else total + term
        return total

    fill_e(list(range(1, CX + 1)))
    total = coarse_taps(1, None)

    @pl.when(has_prev)
    def _():
        for chan in range(n_chan):
            ref = c_buf.at[0, chan]
            rc(ref, ref, hs3.at[0, chan], hr3.at[0, chan], sp - 1, chan).wait_recv()

    @pl.when(has_next)
    def _():
        for chan in range(n_chan):
            ref = c_buf.at[CX + 1, chan]
            rc(ref, ref, hs3.at[1, chan], hr3.at[1, chan], sp + 1, chan).wait_recv()

    fill_e([0, CX + 1])
    total = coarse_taps(0, total)
    total = coarse_taps(2, total)
    rounded = total.astype(BF)
    pb[1] = rounded
    values = rounded.astype(F32)
    pw[1, me] = jnp.sum(values * values, axis=0, keepdims=True)

    for k, chan in enumerate(peers):
        rc(pw.at[1, me], pw.at[1, me], ws4.at[1, k], wr4.at[1, me], sp, chan).start()

    @pl.when(has_next)
    def _():
        rc(pb.at[1], pb.at[0], s4.at[0], r4.at[0], sp + 1, me).start()
        for chan in range(n_chan):
            rc(pw.at[1, me], pw.at[0, me], ws4.at[0, chan], wr4.at[0, me], sp + 1, chan).start()

    @pl.when(has_prev)
    def _():
        rc(pb.at[1], pb.at[2], s4.at[1], r4.at[1], sp - 1, me).start()
        for chan in range(n_chan):
            rc(pw.at[1, me], pw.at[2, me], ws4.at[2, chan], wr4.at[2, me], sp - 1, chan).start()

    own = gain.shape[1]
    gain_col = jnp.sum(
        jnp.where(iota((own, own), 0) == iota((own, own), 1), gain[...], 0.0), axis=1, keepdims=True
    )

    def normed(k):
        power = pw[k, 0]
        for s in range(1, n_chan):
            power = power + pw[k, s]
        scaled = pb[k].astype(F32) * lax.rsqrt(power / coarse + epsilon) * gain_col
        return lax.dot_general(scaled.astype(BF), ohd[k], NT, preferred_element_type=F32)

    for k in range(1, n_chan):
        src = lax.rem(me + k, n_chan)
        rc(pw.at[1, src], pw.at[1, src], ws4.at[1, 0], wr4.at[1, src], sp, src).wait_recv()
    result = normed(1)

    @pl.when(has_prev)
    def _():
        rc(pb.at[0], pb.at[0], s4.at[0], r4.at[0], sp - 1, me).wait_recv()
        for chan in range(n_chan):
            rc(pw.at[0, chan], pw.at[0, chan], ws4.at[0, chan], wr4.at[0, chan], sp - 1, chan).wait_recv()

    @pl.when(has_next)
    def _():
        rc(pb.at[2], pb.at[2], s4.at[1], r4.at[1], sp + 1, me).wait_recv()
        for chan in range(n_chan):
            rc(pw.at[2, chan], pw.at[2, chan], ws4.at[2, chan], wr4.at[2, chan], sp + 1, chan).wait_recv()

    out[...] = (result + normed(0) + normed(2)).astype(BF)

    for x in range(NX):
        for k, chan in enumerate(peers):
            rc(g_buf.at[x + 1, me], g_buf.at[x + 1, me], s2.at[x, k], r2.at[x, me], sp, chan).wait_send()
    for k, chan in enumerate(peers):
        rc(own_c, own_c, s3.at[k], r3.at[me], sp, chan).wait_send()
        rc(pw.at[1, me], pw.at[1, me], ws4.at[1, k], wr4.at[1, me], sp, chan).wait_send()

    @pl.when(has_next)
    def _():
        up_meta.wait_send()
        up_feat.wait_send()
        rc(pb.at[1], pb.at[0], s4.at[0], r4.at[0], sp + 1, me).wait_send()
        for chan in range(n_chan):
            rc(g_buf.at[NX, me], g_buf.at[0, me], hs2.at[chan], hr2.at[me], sp + 1, chan).wait_send()
            rc(c_buf.at[CX, me], c_buf.at[0, me], hs3.at[0, chan], hr3.at[0, me], sp + 1, chan).wait_send()
            rc(pw.at[1, me], pw.at[0, me], ws4.at[0, chan], wr4.at[0, me], sp + 1, chan).wait_send()

    @pl.when(has_prev)
    def _():
        dn_meta.wait_send()
        dn_feat.wait_send()
        rc(pb.at[1], pb.at[2], s4.at[1], r4.at[1], sp - 1, me).wait_send()
        for chan in range(n_chan):
            rc(c_buf.at[1, me], c_buf.at[CX + 1, me], hs3.at[1, chan], hr3.at[1, me], sp - 1, chan).wait_send()
            rc(pw.at[1, me], pw.at[2, me], ws4.at[2, chan], wr4.at[2, me], sp - 1, chan).wait_send()


def body(n_space, n_chan, features, neighbours, parent_index, octant, parent_dest, conv_fine, conv_down, conv_coarse, norm_gain):
    bricks, _, fine = features.shape
    parents = parent_dest.shape[0]
    slots = 2 * parents
    down = conv_down.shape[0]
    own = conv_coarse.shape[0]
    cells = EDGE**3
    coarse = down * n_chan
    vmem = pl.BlockSpec(memory_space=pltpu.VMEM)
    hbm = pl.BlockSpec(memory_space=pltpu.HBM)
    dma = pltpu.SemaphoreType.DMA
    big = n_chan * fine
    crows = CLAYER // (fine // down)
    return pl.pallas_call(
        functools.partial(fused_kernel, n_space, n_chan, bricks, slots),
        out_shape=jax.ShapeDtypeStruct((own, slots * cells), BF),
        in_specs=[hbm] * 12,
        out_specs=vmem,
        scratch_shapes=[
            pltpu.VMEM(features.shape, BF),
            pltpu.VMEM(conv_fine.shape, BF),
            pltpu.VMEM((1, own), F32),
            pltpu.VMEM((1, bricks), jnp.int32),
            pltpu.VMEM((1, bricks), jnp.int32),
            pltpu.VMEM((1, parents), jnp.int32),
            pltpu.VMEM((8, 128), jnp.int32),
            pltpu.VMEM(conv_down.shape, BF),
            pltpu.VMEM(conv_coarse.shape, BF),
            pltpu.VMEM((2, bricks, FACE, fine), BF),
            pltpu.VMEM((2, 8, 128), jnp.int32),
            pltpu.VMEM((NX + 2, LAYER + 2 * NZ, 3 * fine), BF),
            pltpu.VMEM((2, LAYER, fine), F32),
            pltpu.VMEM((NX + 1, n_chan, LAYER // n_chan, fine), BF),
            pltpu.VMEM((big, big), BF),
            pltpu.VMEM((big, big), BF),
            pltpu.VMEM((9 * CLAYER, LAYER), BF),
            pltpu.VMEM((9 * CLAYER, CLAYER), BF),
            pltpu.VMEM((9 * CLAYER, (NX + 1) * fine), BF),
            pltpu.VMEM((CX + 2, n_chan, crows, fine), BF),
            pltpu.VMEM((9 * CLAYER, (CX + 2) * coarse), BF),
            pltpu.VMEM((3, own, parents * cells), BF),
            pltpu.VMEM((3, n_chan, 1, parents * cells), F32),
            pltpu.VMEM((3, slots * cells, parents * cells), BF),
            dma((12,)),
            dma((2, 2)),
            dma((2, 2)),
            dma((NX, n_chan - 1)),
            dma((NX, n_chan)),
            dma((n_chan,)),
            dma((n_chan,)),
            dma((n_chan - 1,)),
            dma((n_chan,)),
            dma((2, n_chan)),
            dma((2, n_chan)),
            dma((2,)),
            dma((2,)),
            dma((3, n_chan)),
            dma((3, n_chan)),
        ],
        compiler_params=pltpu.CompilerParams(collective_id=0, has_side_effects=True, vmem_limit_bytes=66900000
        ),
    )(
        features,
        parent_index.reshape(1, -1),
        octant.reshape(1, -1),
        parent_dest.reshape(1, -1),
        conv_fine,
        conv_down,
        conv_coarse,
        norm_gain.reshape(1, -1),
        *tables(n_chan, fine, down),
    )


def solution(mesh):
    sizes = dict(mesh.shape)
    return jax.shard_map(
        functools.partial(body, sizes["space"], sizes["chan"]),
        mesh=mesh,
        in_specs=(
            P("space", None, None),
            P("space", None),
            P("space"),
            P("space"),
            P("space"),
            P("chan", None),
            P("chan", None),
            P("chan", None),
            P("chan"),
        ),
        out_specs=P("chan", "space"),
        check_vma=False,
    )
```

profile of v0, /device:TPU:0, one launch (start us, length us, event | category | flops | bytes accessed | tf_op | source)
XLA Modules:
  0.0 30.6 jit_solution(12383260367099543921)
XLA Ops:
  0.0 29.1 %shard_map.118 = bf16[64,512]{1,0:T(8,128)(2,1)} custom-call(bf16[16,64,128]{2,1,0:T(8,128)(2,1)} %feat_hbm.1, s32[1,16]{1,0:T(1,128)} %bitcast.4, s32[1,16]{1,0:T(1,128)} %bitcast.5, s32[1,4]{1,0:T(1,128)} %bitcast.6, bf16[32,3456]{1,0:T(8,128)(2,1)} %wf_hbm.1, bf16[64,3456]{1,0:T(8,128)(2,1)} %wd_hbm.1, bf16[64,6912]{1,0:T(8,128)(2,1)} %wc_hbm.1, ...), custom_call_target="tpu_custom_call" | custom-call | tf_op jit(solution)/shard_map/pallas_call | solution.py:524
  29.1 1.5 %copy.14 = bf16[64,512]{1,0:T(8,128)(2,1)} copy(bf16[64,512]{1,0:T(8,128)(2,1)} %shard_map.118) | data formatting | bytes 131072
where the time goes:
time: 31.1 us; the launch traced here: 30.6 us
  Pallas kernels  29.1 us (94%)
  local copies, waits for them, and re-layouts  1.47 us (5%)
    pallas_call x1, Pallas kernels, body(): pl.pallas_call(functools.partial(fused_kernel, n_space, n_chan, bricks, s...  29.1 us
    unnamed x1, local copies, waits for them, and re-layouts  1.47 us

commit v1 on v0

v1 whole, which is shorter than its diff:
```python
import functools

import jax
import jax.numpy as jnp
import numpy as np
from jax import lax
from jax.experimental import pallas as pl
from jax.experimental.pallas import tpu as pltpu
from jax.sharding import PartitionSpec as P

EDGE = 4
SLAB_Y = 4
SLAB_Z = 4
PAD = EDGE + 2
LOW = EDGE + 1
HALF = EDGE // 2
FACE = EDGE * EDGE
CY = SLAB_Y * HALF
CZ = SLAB_Z * HALF
CLAYER = CY * CZ
CX = 2 * HALF
TAPS2 = 9
epsilon = 1e-06
FAR = 1 << 20
BF = jnp.bfloat16
F32 = jnp.float32
NT = (((1,), (1,)), ((), ()))


def iota(shape, dim):
    return lax.broadcasted_iota(jnp.int32, shape, dim)


def one(cond):
    return jnp.where(cond, 1.0, 0.0).astype(BF)


def pick(a, b):
    return jnp.dot(a, b, preferred_element_type=F32)


def tap2(b, c):
    return 3 * (b + 1) + c + 1


def source(pos):
    if pos == 0:
        return -1, EDGE - 1
    if pos == EDGE + 1:
        return 1, 0
    return 0, pos - 1


def table(n_chan, fine):
    wide = fine // n_chan
    r = np.arange(n_chan * EDGE * wide)[:, None]
    q = np.arange(n_chan * EDGE * wide)[None, :]
    group = EDGE * wide
    perm = (r % group) // wide * fine + r // group * wide + r % wide == q
    return jnp.asarray(np.asarray(perm, np.float32).astype(jnp.bfloat16))


def fused_kernel(
    n_space, n_chan, bricks, slots,
    feat_hbm, nbr_hbm, parent_hbm, octant_hbm, dest_hbm, wf_hbm, wd_hbm, wc_hbm, gain_hbm, perm_hbm,
    out,
    feat, nbr, wf, wt, gain, parent_in, octant_in, dest_in, meta, wd, wc, perm,
    fh, mh, pbuf, g_buf, qbuf, c_buf, cp, cn, e_buf, hot_e, hot_o, pb, pw, ohd,
    wsem, s1, r1, s2, r2, hs2, hr2, s3, r3, hs3, hr3, s4, r4, ws4, wr4,
):
    sp = lax.axis_index("space")
    me = lax.axis_index("chan")
    has_prev = sp > 0
    has_next = sp < n_space - 1
    fine = feat.shape[2]
    wide = fine // n_chan
    parents = dest_in.shape[1]
    cells = EDGE**3
    own_d = wd.shape[0]
    coarse = own_d * n_chan
    group = EDGE * wide
    line = EDGE * bricks
    side = HALF * bricks

    def rc(src, dst, ss, rs, space, chan):
        return pltpu.make_async_remote_copy(
            src_ref=src,
            dst_ref=dst,
            send_sem=ss,
            recv_sem=rs,
            device_id={"space": space, "chan": chan},
            device_id_type=pl.DeviceIdType.MESH,
        )

    peers = [lax.rem(me + k, n_chan) for k in range(1, n_chan)]
    barrier = pltpu.get_barrier_semaphore()

    def greet(space, chan):
        pl.semaphore_signal(
            barrier,
            inc=1,
            device_id={"space": space, "chan": chan},
            device_id_type=pl.DeviceIdType.MESH,
        )

    @pl.when(has_prev)
    def _():
        for chan in range(n_chan):
            greet(sp - 1, chan)

    @pl.when(has_next)
    def _():
        for chan in range(n_chan):
            greet(sp + 1, chan)

    for chan in peers:
        greet(sp, chan)

    loads = [
        pltpu.make_async_copy(src, dst, wsem.at[k])
        for k, (src, dst) in enumerate(
            (
                (nbr_hbm, nbr),
                (feat_hbm, feat),
                (parent_hbm, parent_in),
                (octant_hbm, octant_in),
                (dest_hbm, dest_in),
                (wf_hbm, wf),
                (perm_hbm, perm),
                (wd_hbm, wd),
                (gain_hbm, gain),
                (wc_hbm, wc),
            )
        )
    ]
    for load in loads:
        load.start()

    @pl.when(jnp.logical_not(has_prev))
    def _():
        fh[0] = jnp.zeros(fh.shape[1:], BF)
        mh[0] = jnp.zeros(mh.shape[1:], jnp.int32)
        for s in range(n_chan):
            g_buf[s, 0] = jnp.zeros(g_buf.shape[2:], BF)
        cp[...] = jnp.zeros(cp.shape, BF)
        pb[0] = jnp.zeros(pb.shape[1:], BF)
        pw[0] = jnp.zeros(pw.shape[1:], F32)

    @pl.when(jnp.logical_not(has_next))
    def _():
        fh[1] = jnp.zeros(fh.shape[1:], BF)
        mh[1] = jnp.zeros(mh.shape[1:], jnp.int32)
        cn[...] = jnp.zeros(cn.shape, BF)
        pb[2] = jnp.zeros(pb.shape[1:], BF)
        pw[2] = jnp.zeros(pw.shape[1:], F32)

    reach = PAD * fine
    for z in range(EDGE):
        for bc in range(TAPS2):
            at = bc * reach
            rows = slice(z * wide, (z + 1) * wide)
            if z > 0:
                wt[rows, at : at + z * fine] = jnp.zeros((wide, z * fine), BF)
            if z < EDGE - 1:
                wt[rows, at + (z + 3) * fine : at + reach] = jnp.zeros((wide, (EDGE - 1 - z) * fine), BF)
    meta[...] = jnp.zeros(meta.shape, jnp.int32)

    for load in loads[2:5]:
        load.wait()
    local = parent_in[...] - sp * parents
    octant = octant_in[...]
    y_pos = 2 * (local // (SLAB_Z // 2)) + octant // 2 % 2
    z_pos = 2 * (local % (SLAB_Z // 2)) + octant // 4
    meta[0:1, 0:bricks] = octant % 2 + 2 * y_pos + 2 * SLAB_Y * z_pos
    meta[1:2, 0:parents] = dest_in[...] - (sp - 1) * slots

    up_feat = rc(feat_hbm.at[:, pl.ds((EDGE - 1) * FACE, FACE), :], fh.at[0], s1.at[0, 0], r1.at[0, 0], sp + 1, me)
    up_meta = rc(meta, mh.at[0], s1.at[0, 1], r1.at[0, 1], sp + 1, me)
    dn_feat = rc(feat_hbm.at[:, pl.ds(0, FACE), :], fh.at[1], s1.at[1, 0], r1.at[1, 0], sp - 1, me)
    dn_meta = rc(meta, mh.at[1], s1.at[1, 1], r1.at[1, 1], sp - 1, me)

    pl.semaphore_wait(
        barrier, n_chan - 1 + n_chan * (has_prev.astype(jnp.int32) + has_next.astype(jnp.int32))
    )

    @pl.when(has_next)
    def _():
        up_feat.start()
        up_meta.start()

    @pl.when(has_prev)
    def _():
        dn_feat.start()
        dn_meta.start()

    for load in loads[0:2]:
        load.wait()
    raw = nbr[...]
    loc = jnp.where(raw >= 0, raw - bricks * (sp - 1), -FAR)
    here = iota((bricks, 1), 0) + bricks

    def loc_of(a, b, c):
        k = 9 * (a + 1) + tap2(b, c)
        if k == 13:
            return here
        k = k - (k > 13)
        return loc[:, k : k + 1]

    def place(a, first, sources, planes):
        wide_k = sources.shape[0]
        col = iota((bricks, wide_k), 1)
        keys = {
            (b, c): jnp.broadcast_to((loc_of(a, b, c) - first) * FACE, (bricks, wide_k))
            for b in (-1, 0, 1)
            for c in (-1, 0, 1)
        }
        for zq in range(PAD):
            c, sz = source(zq)
            hots = []
            for yq in range(PAD):
                b, sy = source(yq)
                hots.append(one(col == keys[b, c] + (sy * EDGE + sz)))
            placed = pick(jnp.concatenate(hots, axis=0), sources).astype(BF)
            for i, xq in enumerate(planes):
                pbuf[xq, :, :, zq * fine : (zq + 1) * fine] = placed[:, i * fine : (i + 1) * fine].reshape(
                    PAD, bricks, fine
                )

    def plane(i):
        return feat[:, i * FACE : (i + 1) * FACE, :].reshape(bricks * FACE, fine)

    place(0, bricks, jnp.concatenate([plane(i) for i in range(EDGE)], axis=1), range(1, EDGE + 1))

    loads[5].wait()
    for z in range(EDGE):
        for bc in range(TAPS2):
            at = bc * reach + z * fine
            wt[z * wide : (z + 1) * wide, at : at + 3 * fine] = wf[:, bc * 3 * fine : (bc + 1) * 3 * fine]

    def hidden(planes):
        parts = []
        for a in range(3):
            for b in range(3):
                parts.append(
                    jnp.concatenate([pbuf[x + a, b : b + EDGE].reshape(line, reach) for x in planes], axis=0)
                )
        total = lax.dot_general(jnp.concatenate(parts, axis=1), wt[...], NT, preferred_element_type=F32)
        total = jnp.maximum(total, 0.0).astype(BF)
        for i, x in enumerate(planes):
            g_buf[me, x + 1] = total[i * line : (i + 1) * line]

    spans = ((2, EDGE - 2), (EDGE, 1), (1, 1))

    def hid_copy(j, k, chan):
        ref = g_buf.at[me, pl.ds(*spans[j])]
        return rc(ref, ref, s2.at[j, k], r2.at[j, me], sp, chan)

    def hid_wait(j):
        for k in range(1, n_chan):
            src = lax.rem(me + k, n_chan)
            ref = g_buf.at[src, pl.ds(*spans[j])]
            rc(ref, ref, s2.at[j, 0], r2.at[j, src], sp, src).wait_recv()

    hidden(list(range(1, EDGE - 1)))
    for k, chan in enumerate(peers):
        hid_copy(0, k, chan).start()

    @pl.when(has_next)
    def _():
        dn_feat.wait_recv()
        dn_meta.wait_recv()

    place(1, bricks, jnp.concatenate([plane(0), fh[1].reshape(bricks * FACE, fine)], axis=0), [EDGE + 1])

    @pl.when(has_prev)
    def _():
        up_feat.wait_recv()
        up_meta.wait_recv()

    place(-1, 0, jnp.concatenate([fh[0].reshape(bricks * FACE, fine), plane(EDGE - 1)], axis=0), [0])
    hidden([0, EDGE - 1])

    @pl.when(has_next)
    def _():
        for chan in range(n_chan):
            rc(g_buf.at[me, EDGE], g_buf.at[me, 0], hs2.at[chan], hr2.at[me], sp + 1, chan).start()

    for j in (1, 2):
        for k, chan in enumerate(peers):
            hid_copy(j, k, chan).start()

    lanes = meta.shape[1]
    lane_par = jnp.where(
        iota((lanes, parents * cells), 1) // cells == iota((lanes, parents * cells), 0), 1.0, 0.0
    )

    def dest_table(k):
        block = meta[...] if k == 1 else mh[k // 2]
        rel = jnp.dot(block.astype(F32), lane_par, preferred_element_type=F32)[1:2].astype(jnp.int32)
        slot = rel - (2 - k) * slots
        target = slot * cells + iota((1, parents * cells), 1) % cells
        ids = iota((slots * cells, parents * cells), 0)
        ohd[k] = one(ids == jnp.where((slot >= 0) & (slot < slots), target, -1))

    n_own = HALF**3 * bricks
    spread = jnp.where(iota((lanes, n_own), 1) % bricks == iota((lanes, n_own), 0), 1.0, 0.0)

    def codes(block, n):
        code = jnp.dot(block.astype(F32), spread[:, 0:n], preferred_element_type=F32)[0:1].astype(jnp.int32)
        return code % 2, code // 2 % SLAB_Y, code // (2 * SLAB_Y)

    def wants(n, bc):
        at = iota((CLAYER, n), 0)
        par, yz = at // FACE, at % FACE
        y = par // (SLAB_Z // 2) * EDGE + yz // EDGE + bc // 3 - 1
        z = par % (SLAB_Z // 2) * EDGE + yz % EDGE + bc % 3 - 1
        return jnp.where((y >= 0) & (y < CY) & (z >= 0) & (z < CZ), y * CZ + z, FAR)

    x_bit, y_at, z_at = codes(meta[...], n_own)
    sub = iota((1, n_own), 1) // bricks
    key = (2 * y_at + sub % HALF) * CZ + 2 * z_at + sub // (HALF * HALF)
    layer = 2 * x_bit + sub // HALF % HALF
    for bc in range(TAPS2):
        want = wants(n_own, bc)
        for x in range(CX):
            hot_e[x, bc * CLAYER : (bc + 1) * CLAYER] = one(want == jnp.where(layer == x, key, -1))

    n_out = HALF * HALF * bricks
    for k in range(2):
        x_bit, y_at, z_at = codes(mh[k], n_out)
        sub = iota((1, n_out), 1) // bricks
        key = (2 * y_at + sub % HALF) * CZ + 2 * z_at + sub // HALF
        key = jnp.where(x_bit == 1 - k, key, -1)
        for bc in range(TAPS2):
            hot_o[k, bc * CLAYER : (bc + 1) * CLAYER] = one(wants(n_out, bc) == key)

    for k in range(3):
        dest_table(k)

    for load in loads[6:8]:
        load.wait()

    for j in range(3):
        hid_wait(j)

    def unpack(first, number):
        joined = jnp.concatenate(
            [g_buf[s, first : first + number].reshape(number * line, group) for s in range(n_chan)], axis=1
        )
        return pick(joined, perm[...]).astype(BF)

    full = EDGE * fine
    moved = unpack(1, EDGE)
    for x in range(EDGE):
        qbuf[x + 1, 1:LOW, :, fine : LOW * fine] = moved[x * line : (x + 1) * line].reshape(EDGE, bricks, full)

    def hot_rows(a, c, n):
        col = iota((bricks, n), 1)
        rows = []
        for yq in range(LOW):
            b, sy = source(yq)
            where = loc_of(a, b, c)
            where = jnp.where(where >= bricks, where - bricks, where + line) + sy * bricks
            rows.append(one(col == where))
        return jnp.concatenate(rows, axis=0)

    tail = fine * (EDGE - 1)
    edge_y = pick(
        one(iota((bricks, bricks), 1) == loc_of(0, -1, 0) - bricks),
        jnp.concatenate([moved[x * line + line - bricks : (x + 1) * line] for x in range(EDGE)], axis=1),
    ).astype(BF)
    edge_z = pick(
        hot_rows(0, -1, line), jnp.concatenate([moved[x * line : (x + 1) * line, tail:] for x in range(EDGE)], axis=1)
    ).astype(BF)
    for x in range(EDGE):
        qbuf[x + 1, 0, :, fine : LOW * fine] = edge_y[:, x * full : (x + 1) * full]
        qbuf[x + 1, :, :, 0:fine] = edge_z[:, x * fine : (x + 1) * fine].reshape(LOW, bricks, fine)

    @pl.when(has_prev)
    def _():
        for chan in range(n_chan):
            rc(g_buf.at[chan, 0], g_buf.at[chan, 0], hs2.at[chan], hr2.at[chan], sp - 1, chan).wait_recv()

    joint = jnp.concatenate([moved[tail // fine * line :], unpack(0, 1)], axis=0)
    qbuf[0, :, :, fine : LOW * fine] = pick(hot_rows(-1, 0, 2 * line), joint).astype(BF).reshape(LOW, bricks, full)
    qbuf[0, :, :, 0:fine] = pick(hot_rows(-1, -1, 2 * line), joint[:, tail:]).astype(BF).reshape(LOW, bricks, fine)

    stacked = []
    for qz in range(HALF):
        for qx in range(HALF):
            for qy in range(HALF):
                stacked.append(
                    jnp.concatenate(
                        [
                            qbuf[2 * qx + a, 2 * qy + b, :, 2 * qz * fine : (2 * qz + 3) * fine]
                            for a in range(3)
                            for b in range(3)
                        ],
                        axis=1,
                    )
                )
    pieces = lax.dot_general(jnp.concatenate(stacked, axis=0), wd[...], NT, preferred_element_type=F32)
    pieces = jnp.maximum(pieces, 0.0)
    part = 2 * side
    c_buf[me] = jnp.concatenate([pieces[h * part : (h + 1) * part] for h in range(HALF)], axis=1).astype(BF)

    for k, chan in enumerate(peers):
        rc(c_buf.at[me], c_buf.at[me], s3.at[k], r3.at[me], sp, chan).start()

    @pl.when(has_next)
    def _():
        for chan in range(n_chan):
            rc(c_buf.at[me, pl.ds(side, side)], cp.at[me], hs3.at[0, chan], hr3.at[0, me], sp + 1, chan).start()

    @pl.when(has_prev)
    def _():
        for chan in range(n_chan):
            rc(c_buf.at[me, pl.ds(0, side)], cn.at[me], hs3.at[1, chan], hr3.at[1, me], sp - 1, chan).start()

    for load in loads[8:]:
        load.wait()
    own = gain.shape[1]
    gain_col = jnp.sum(
        jnp.where(iota((own, own), 0) == iota((own, own), 1), gain[...], 0.0), axis=1, keepdims=True
    )

    for k in range(1, n_chan):
        src = lax.rem(me + k, n_chan)
        rc(c_buf.at[src], c_buf.at[src], s3.at[0], r3.at[src], sp, src).wait_recv()

    def all_channels(buf):
        return jnp.concatenate(
            [
                jnp.concatenate([buf[s][:, h * own_d : (h + 1) * own_d] for s in range(n_chan)], axis=1)
                for h in range(HALF)
            ],
            axis=0,
        )

    def coarse_taps(a, total):
        for bc in range(TAPS2):
            block = jnp.concatenate(
                [
                    e_buf[x + a, bc * CLAYER + g * FACE : bc * CLAYER + (g + 1) * FACE, :]
                    for g in range(parents)
                    for x in range(CX)
                ],
                axis=0,
            )
            t = a * TAPS2 + bc
            term = lax.dot_general(wc[:, t * coarse : (t + 1) * coarse], block, NT, preferred_element_type=F32)
            total = term if total is None else total + term
        return total

    inside = all_channels(c_buf)
    for x in range(CX):
        e_buf[x + 1] = pick(hot_e[x], inside).astype(BF)
    total = coarse_taps(1, None)

    @pl.when(has_prev)
    def _():
        for chan in range(n_chan):
            rc(cp.at[chan], cp.at[chan], hs3.at[0, chan], hr3.at[0, chan], sp - 1, chan).wait_recv()

    @pl.when(has_next)
    def _():
        for chan in range(n_chan):
            rc(cn.at[chan], cn.at[chan], hs3.at[1, chan], hr3.at[1, chan], sp + 1, chan).wait_recv()

    e_buf[0] = pick(hot_o[0], all_channels(cp)).astype(BF)
    e_buf[CX + 1] = pick(hot_o[1], all_channels(cn)).astype(BF)
    total = coarse_taps(0, total)
    total = coarse_taps(2, total)
    rounded = total.astype(BF)
    pb[1] = rounded
    values = rounded.astype(F32)
    pw[1, me] = jnp.sum(values * values, axis=0, keepdims=True)

    for k, chan in enumerate(peers):
        rc(pw.at[1, me], pw.at[1, me], ws4.at[1, k], wr4.at[1, me], sp, chan).start()

    @pl.when(has_next)
    def _():
        rc(pb.at[1], pb.at[0], s4.at[0], r4.at[0], sp + 1, me).start()
        for chan in range(n_chan):
            rc(pw.at[1, me], pw.at[0, me], ws4.at[0, chan], wr4.at[0, me], sp + 1, chan).start()

    @pl.when(has_prev)
    def _():
        rc(pb.at[1], pb.at[2], s4.at[1], r4.at[1], sp - 1, me).start()
        for chan in range(n_chan):
            rc(pw.at[1, me], pw.at[2, me], ws4.at[2, chan], wr4.at[2, me], sp - 1, chan).start()

    def normed(k):
        power = pw[k, 0]
        for s in range(1, n_chan):
            power = power + pw[k, s]
        scaled = pb[k].astype(F32) * lax.rsqrt(power / coarse + epsilon) * gain_col
        return lax.dot_general(scaled.astype(BF), ohd[k], NT, preferred_element_type=F32)

    for k in range(1, n_chan):
        src = lax.rem(me + k, n_chan)
        rc(pw.at[1, src], pw.at[1, src], ws4.at[1, 0], wr4.at[1, src], sp, src).wait_recv()
    result = normed(1)

    @pl.when(has_prev)
    def _():
        rc(pb.at[0], pb.at[0], s4.at[0], r4.at[0], sp - 1, me).wait_recv()
        for chan in range(n_chan):
            rc(pw.at[0, chan], pw.at[0, chan], ws4.at[0, chan], wr4.at[0, chan], sp - 1, chan).wait_recv()

    @pl.when(has_next)
    def _():
        rc(pb.at[2], pb.at[2], s4.at[1], r4.at[1], sp + 1, me).wait_recv()
        for chan in range(n_chan):
            rc(pw.at[2, chan], pw.at[2, chan], ws4.at[2, chan], wr4.at[2, chan], sp + 1, chan).wait_recv()

    out[...] = (result + normed(0) + normed(2)).astype(BF)

    for k, chan in enumerate(peers):
        for j in range(3):
            hid_copy(j, k, chan).wait_send()
        rc(c_buf.at[me], c_buf.at[me], s3.at[k], r3.at[me], sp, chan).wait_send()
        rc(pw.at[1, me], pw.at[1, me], ws4.at[1, k], wr4.at[1, me], sp, chan).wait_send()

    @pl.when(has_next)
    def _():
        up_meta.wait_send()
        up_feat.wait_send()
        rc(pb.at[1], pb.at[0], s4.at[0], r4.at[0], sp + 1, me).wait_send()
        for chan in range(n_chan):
            rc(g_buf.at[me, EDGE], g_buf.at[me, 0], hs2.at[chan], hr2.at[me], sp + 1, chan).wait_send()
            rc(c_buf.at[me, pl.ds(side, side)], cp.at[me], hs3.at[0, chan], hr3.at[0, me], sp + 1, chan).wait_send()
            rc(pw.at[1, me], pw.at[0, me], ws4.at[0, chan], wr4.at[0, me], sp + 1, chan).wait_send()

    @pl.when(has_prev)
    def _():
        dn_meta.wait_send()
        dn_feat.wait_send()
        rc(pb.at[1], pb.at[2], s4.at[1], r4.at[1], sp - 1, me).wait_send()
        for chan in range(n_chan):
            rc(c_buf.at[me, pl.ds(0, side)], cn.at[me], hs3.at[1, chan], hr3.at[1, me], sp - 1, chan).wait_send()
            rc(pw.at[1, me], pw.at[2, me], ws4.at[2, chan], wr4.at[2, me], sp - 1, chan).wait_send()


def body(n_space, n_chan, features, neighbours, parent_index, octant, parent_dest, conv_fine, conv_down, conv_coarse, norm_gain):
    bricks, _, fine = features.shape
    parents = parent_dest.shape[0]
    slots = 2 * parents
    own_d = conv_down.shape[0]
    own = conv_coarse.shape[0]
    cells = EDGE**3
    coarse = own_d * n_chan
    group = EDGE * fine // n_chan
    vmem = pl.BlockSpec(memory_space=pltpu.VMEM)
    hbm = pl.BlockSpec(memory_space=pltpu.HBM)
    dma = pltpu.SemaphoreType.DMA
    return pl.pallas_call(
        functools.partial(fused_kernel, n_space, n_chan, bricks, slots),
        out_shape=jax.ShapeDtypeStruct((own, slots * cells), BF),
        in_specs=[hbm] * 10,
        out_specs=vmem,
        scratch_shapes=[
            pltpu.VMEM(features.shape, BF),
            pltpu.VMEM(neighbours.shape, jnp.int32),
            pltpu.VMEM(conv_fine.shape, BF),
            pltpu.VMEM((group, TAPS2 * PAD * fine), BF),
            pltpu.VMEM((1, own), F32),
            pltpu.VMEM((1, bricks), jnp.int32),
            pltpu.VMEM((1, bricks), jnp.int32),
            pltpu.VMEM((1, parents), jnp.int32),
            pltpu.VMEM((8, 128), jnp.int32),
            pltpu.VMEM(conv_down.shape, BF),
            pltpu.VMEM(conv_coarse.shape, BF),
            pltpu.VMEM((n_chan * group, n_chan * group), BF),
            pltpu.VMEM((2, bricks, FACE, fine), BF),
            pltpu.VMEM((2, 8, 128), jnp.int32),
            pltpu.VMEM((PAD, PAD, bricks, PAD * fine), BF),
            pltpu.VMEM((n_chan, LOW, EDGE * bricks, group), BF),
            pltpu.VMEM((LOW, LOW, bricks, LOW * fine), BF),
            pltpu.VMEM((n_chan, HALF * HALF * bricks, HALF * own_d), BF),
            pltpu.VMEM((n_chan, HALF * bricks, HALF * own_d), BF),
            pltpu.VMEM((n_chan, HALF * bricks, HALF * own_d), BF),
            pltpu.VMEM((CX + 2, TAPS2 * CLAYER, coarse), BF),
            pltpu.VMEM((CX, TAPS2 * CLAYER, HALF**3 * bricks), BF),
            pltpu.VMEM((2, TAPS2 * CLAYER, HALF**2 * bricks), BF),
            pltpu.VMEM((3, own, parents * cells), BF),
            pltpu.VMEM((3, n_chan, 1, parents * cells), F32),
            pltpu.VMEM((3, slots * cells, parents * cells), BF),
            dma((10,)),
            dma((2, 2)),
            dma((2, 2)),
            dma((3, n_chan - 1)),
            dma((3, n_chan)),
            dma((n_chan,)),
            dma((n_chan,)),
            dma((n_chan - 1,)),
            dma((n_chan,)),
            dma((2, n_chan)),
            dma((2, n_chan)),
            dma((2,)),
            dma((2,)),
            dma((3, n_chan)),
            dma((3, n_chan)),
        ],
        compiler_params=pltpu.CompilerParams(
            collective_id=0, has_side_effects=True, vmem_limit_bytes=66900000
        ),
    )(
        features,
        neighbours,
        parent_index.reshape(1, -1),
        octant.reshape(1, -1),
        parent_dest.reshape(1, -1),
        conv_fine,
        conv_down,
        conv_coarse,
        norm_gain.reshape(1, -1),
        table(n_chan, fine),
    )


def solution(mesh):
    sizes = dict(mesh.shape)
    return jax.shard_map(
        functools.partial(body, sizes["space"], sizes["chan"]),
        mesh=mesh,
        in_specs=(
            P("space", None, None),
            P("space", None),
            P("space"),
            P("space"),
            P("space"),
            P("chan", None),
            P("chan", None),
            P("chan", None),
            P("chan"),
        ),
        out_specs=P("chan", "space"),
        check_vma=False,
    )
```

time: 31.1 us -> 29.4 us (0.945); the launches traced: 30.6 us -> 29.3 us
  Pallas kernels: 29.1 us -> 27.8 us
    pallas_call x1, Pallas kernels: 29.1 us -> 27.8 us  [body(): pl.pallas_call(functools.partial(fused_kernel, n_space, n_chan, bricks, s...]
where the time goes in v1:
time: 29.4 us; the launch traced here: 29.3 us
  Pallas kernels  27.8 us (95%)
  local copies, waits for them, and re-layouts  1.47 us (5%)
    pallas_call x1, Pallas kernels, body(): pl.pallas_call(functools.partial(fused_kernel, n_space, n_chan, bricks, s...  27.8 us
    unnamed x1, local copies, waits for them, and re-layouts  1.47 us

profile of v1, /device:TPU:0, one launch (start us, length us, event | category | flops | bytes accessed | tf_op | source)
XLA Modules:
  0.0 29.3 jit_solution(12040080533802957166)
XLA Ops:
  0.0 27.8 %shard_map.100 = bf16[64,512]{1,0:T(8,128)(2,1)} custom-call(bf16[16,64,128]{2,1,0:T(8,128)(2,1)} %feat_hbm.1, s32[16,26]{1,0:T(8,128)} %nbr_hbm.1, s32[1,16]{1,0:T(1,128)} %bitcast.4, s32[1,16]{1,0:T(1,128)} %bitcast.5, s32[1,4]{1,0:T(1,128)} %bitcast.6, bf16[32,3456]{1,0:T(8,128)(2,1)} %wf_hbm.1, bf16[64,3456]{1,0:T(8,128)(2,1)} %wd_hbm.1, ...), custom_call_target="tpu_custom_call" | custom-call | tf_op jit(solution)/shard_map/pallas_call | solution.py:558
  27.8 1.5 %copy.12 = bf16[64,512]{1,0:T(8,128)(2,1)} copy(bf16[64,512]{1,0:T(8,128)(2,1)} %shard_map.100) | data formatting | bytes 131072

commit v2 on v1

--- a/solution.py
+++ b/solution.py
@@ -65,7 +65,7 @@
     feat_hbm, nbr_hbm, parent_hbm, octant_hbm, dest_hbm, wf_hbm, wd_hbm, wc_hbm, gain_hbm, perm_hbm,
     out,
     feat, nbr, wf, wt, gain, parent_in, octant_in, dest_in, meta, wd, wc, perm,
-    fh, mh, pbuf, g_buf, qbuf, c_buf, cp, cn, e_buf, hot_e, hot_o, pb, pw, ohd,
+    fh, mh, pbuf, part_h, g_buf, qbuf, c_buf, cp, cn, e_buf, hot_e, hot_o, pb, pw, ohd,
     wsem, s1, r1, s2, r2, hs2, hr2, s3, r3, hs3, hr3, s4, r4, ws4, wr4,
 ):
     sp = lax.axis_index("space")
@@ -105,13 +105,11 @@
 
     @pl.when(has_prev)
     def _():
-        for chan in range(n_chan):
-            greet(sp - 1, chan)
-
-    @pl.when(has_next)
-    def _():
-        for chan in range(n_chan):
-            greet(sp + 1, chan)
+        greet(sp - 1, me)
+
+    @pl.when(has_next)
+    def _():
+        greet(sp + 1, me)
 
     for chan in peers:
         greet(sp, chan)
@@ -136,6 +134,21 @@
     for load in loads:
         load.start()
 
+    up_feat = rc(feat_hbm.at[:, pl.ds((EDGE - 1) * FACE, FACE), :], fh.at[0], s1.at[0, 0], r1.at[0, 0], sp + 1, me)
+    up_meta = rc(meta, mh.at[0], s1.at[0, 1], r1.at[0, 1], sp + 1, me)
+    dn_feat = rc(feat_hbm.at[:, pl.ds(0, FACE), :], fh.at[1], s1.at[1, 0], r1.at[1, 0], sp - 1, me)
+    dn_meta = rc(meta, mh.at[1], s1.at[1, 1], r1.at[1, 1], sp - 1, me)
+
+    pl.semaphore_wait(barrier, n_chan - 1 + has_prev.astype(jnp.int32) + has_next.astype(jnp.int32))
+
+    @pl.when(has_next)
+    def _():
+        up_feat.start()
+
+    @pl.when(has_prev)
+    def _():
+        dn_feat.start()
+
     @pl.when(jnp.logical_not(has_prev))
     def _():
         fh[0] = jnp.zeros(fh.shape[1:], BF)
@@ -174,23 +187,12 @@
     meta[0:1, 0:bricks] = octant % 2 + 2 * y_pos + 2 * SLAB_Y * z_pos
     meta[1:2, 0:parents] = dest_in[...] - (sp - 1) * slots
 
-    up_feat = rc(feat_hbm.at[:, pl.ds((EDGE - 1) * FACE, FACE), :], fh.at[0], s1.at[0, 0], r1.at[0, 0], sp + 1, me)
-    up_meta = rc(meta, mh.at[0], s1.at[0, 1], r1.at[0, 1], sp + 1, me)
-    dn_feat = rc(feat_hbm.at[:, pl.ds(0, FACE), :], fh.at[1], s1.at[1, 0], r1.at[1, 0], sp - 1, me)
-    dn_meta = rc(meta, mh.at[1], s1.at[1, 1], r1.at[1, 1], sp - 1, me)
-
-    pl.semaphore_wait(
-        barrier, n_chan - 1 + n_chan * (has_prev.astype(jnp.int32) + has_next.astype(jnp.int32))
-    )
-
-    @pl.when(has_next)
-    def _():
-        up_feat.start()
+    @pl.when(has_next)
+    def _():
         up_meta.start()
 
     @pl.when(has_prev)
     def _():
-        dn_feat.start()
         dn_meta.start()
 
     for load in loads[0:2]:
@@ -230,6 +232,8 @@
         return feat[:, i * FACE : (i + 1) * FACE, :].reshape(bricks * FACE, fine)
 
     place(0, bricks, jnp.concatenate([plane(i) for i in range(EDGE)], axis=1), range(1, EDGE + 1))
+    place(-1, bricks, plane(EDGE - 1), [0])
+    place(1, bricks, plane(0), [EDGE + 1])
 
     loads[5].wait()
     for z in range(EDGE):
@@ -237,17 +241,26 @@
             at = bc * reach + z * fine
             wt[z * wide : (z + 1) * wide, at : at + 3 * fine] = wf[:, bc * 3 * fine : (bc + 1) * 3 * fine]
 
-    def hidden(planes):
-        parts = []
-        for a in range(3):
-            for b in range(3):
-                parts.append(
-                    jnp.concatenate([pbuf[x + a, b : b + EDGE].reshape(line, reach) for x in planes], axis=0)
-                )
-        total = lax.dot_general(jnp.concatenate(parts, axis=1), wt[...], NT, preferred_element_type=F32)
-        total = jnp.maximum(total, 0.0).astype(BF)
-        for i, x in enumerate(planes):
-            g_buf[me, x + 1] = total[i * line : (i + 1) * line]
+    def cube(x, b):
+        return pbuf[x, b : b + EDGE].reshape(line, reach)
+
+    parts = []
+    for a in range(3):
+        for b in range(3):
+            parts.append(jnp.concatenate([cube(x + a, b) for x in range(EDGE)], axis=0))
+    total = lax.dot_general(jnp.concatenate(parts, axis=1), wt[...], NT, preferred_element_type=F32)
+    part_h[0] = total[0:line]
+    part_h[1] = total[(EDGE - 1) * line :]
+    for x in range(1, EDGE - 1):
+        g_buf[me, x + 1] = jnp.maximum(total[x * line : (x + 1) * line], 0.0).astype(BF)
+
+    def finish(k, a, first, x, xq):
+        place(a, first, fh[k].reshape(bricks * FACE, fine), [xq])
+        taps = wt[:, (a + 1) * 3 * reach : (a + 2) * 3 * reach]
+        rest = lax.dot_general(
+            jnp.concatenate([cube(xq, b) for b in range(3)], axis=1), taps, NT, preferred_element_type=F32
+        )
+        g_buf[me, x + 1] = jnp.maximum(part_h[k] + rest, 0.0).astype(BF)
 
     spans = ((2, EDGE - 2), (EDGE, 1), (1, 1))
 
@@ -261,33 +274,37 @@
             ref = g_buf.at[src, pl.ds(*spans[j])]
             rc(ref, ref, s2.at[j, 0], r2.at[j, src], sp, src).wait_recv()
 
-    hidden(list(range(1, EDGE - 1)))
     for k, chan in enumerate(peers):
         hid_copy(0, k, chan).start()
 
     @pl.when(has_next)
     def _():
         dn_feat.wait_recv()
+
+    finish(1, 1, 2 * bricks, EDGE - 1, EDGE + 1)
+    for k, chan in enumerate(peers):
+        hid_copy(1, k, chan).start()
+
+    @pl.when(has_next)
+    def _():
+        for chan in range(n_chan):
+            rc(g_buf.at[me, EDGE], g_buf.at[me, 0], hs2.at[chan], hr2.at[me], sp + 1, chan).start()
+
+    @pl.when(has_prev)
+    def _():
+        up_feat.wait_recv()
+
+    finish(0, -1, 0, 0, 0)
+    for k, chan in enumerate(peers):
+        hid_copy(2, k, chan).start()
+
+    @pl.when(has_next)
+    def _():
         dn_meta.wait_recv()
 
-    place(1, bricks, jnp.concatenate([plane(0), fh[1].reshape(bricks * FACE, fine)], axis=0), [EDGE + 1])
-
-    @pl.when(has_prev)
-    def _():
-        up_feat.wait_recv()
+    @pl.when(has_prev)
+    def _():
         up_meta.wait_recv()
-
-    place(-1, 0, jnp.concatenate([fh[0].reshape(bricks * FACE, fine), plane(EDGE - 1)], axis=0), [0])
-    hidden([0, EDGE - 1])
-
-    @pl.when(has_next)
-    def _():
-        for chan in range(n_chan):
-            rc(g_buf.at[me, EDGE], g_buf.at[me, 0], hs2.at[chan], hr2.at[me], sp + 1, chan).start()
-
-    for j in (1, 2):
-        for k, chan in enumerate(peers):
-            hid_copy(j, k, chan).start()
 
     lanes = meta.shape[1]
     lane_par = jnp.where(
@@ -437,25 +454,27 @@
             axis=0,
         )
 
-    def coarse_taps(a, total):
+    def coarse_taps(a):
+        blocks = []
         for bc in range(TAPS2):
-            block = jnp.concatenate(
-                [
-                    e_buf[x + a, bc * CLAYER + g * FACE : bc * CLAYER + (g + 1) * FACE, :]
-                    for g in range(parents)
-                    for x in range(CX)
-                ],
-                axis=0,
+            blocks.append(
+                jnp.concatenate(
+                    [
+                        e_buf[x + a, bc * CLAYER + g * FACE : bc * CLAYER + (g + 1) * FACE, :]
+                        for g in range(parents)
+                        for x in range(CX)
+                    ],
+                    axis=0,
+                )
             )
-            t = a * TAPS2 + bc
-            term = lax.dot_general(wc[:, t * coarse : (t + 1) * coarse], block, NT, preferred_element_type=F32)
-            total = term if total is None else total + term
-        return total
+        span = TAPS2 * coarse
+        taps = wc[:, a * span : (a + 1) * span]
+        return lax.dot_general(taps, jnp.concatenate(blocks, axis=1), NT, preferred_element_type=F32)
 
     inside = all_channels(c_buf)
     for x in range(CX):
         e_buf[x + 1] = pick(hot_e[x], inside).astype(BF)
-    total = coarse_taps(1, None)
+    total = coarse_taps(1)
 
     @pl.when(has_prev)
     def _():
@@ -469,8 +488,7 @@
 
     e_buf[0] = pick(hot_o[0], all_channels(cp)).astype(BF)
     e_buf[CX + 1] = pick(hot_o[1], all_channels(cn)).astype(BF)
-    total = coarse_taps(0, total)
-    total = coarse_taps(2, total)
+    total = total + coarse_taps(0) + coarse_taps(2)
     rounded = total.astype(BF)
     pb[1] = rounded
     values = rounded.astype(F32)
@@ -555,6 +573,10 @@
     vmem = pl.BlockSpec(memory_space=pltpu.VMEM)
     hbm = pl.BlockSpec(memory_space=pltpu.HBM)
     dma = pltpu.SemaphoreType.DMA
+
+    def fixed(x):
+        return pltpu.with_memory_space_constraint(x, pltpu.HBM)
+
     return pl.pallas_call(
         functools.partial(fused_kernel, n_space, n_chan, bricks, slots),
         out_shape=jax.ShapeDtypeStruct((own, slots * cells), BF),
@@ -576,6 +598,7 @@
             pltpu.VMEM((2, bricks, FACE, fine), BF),
             pltpu.VMEM((2, 8, 128), jnp.int32),
             pltpu.VMEM((PAD, PAD, bricks, PAD * fine), BF),
+            pltpu.VMEM((2, EDGE * bricks, group), F32),
             pltpu.VMEM((n_chan, LOW, EDGE * bricks, group), BF),
             pltpu.VMEM((LOW, LOW, bricks, LOW * fine), BF),
             pltpu.VMEM((n_chan, HALF * HALF * bricks, HALF * own_d), BF),
@@ -604,19 +627,19 @@
             dma((3, n_chan)),
         ],
         compiler_params=pltpu.CompilerParams(
-            collective_id=0, has_side_effects=True, vmem_limit_bytes=66900000
+            collective_id=0, has_side_effects=True, vmem_limit_bytes=40000000
         ),
     )(
-        features,
-        neighbours,
-        parent_index.reshape(1, -1),
-        octant.reshape(1, -1),
-        parent_dest.reshape(1, -1),
-        conv_fine,
-        conv_down,
-        conv_coarse,
-        norm_gain.reshape(1, -1),
-        table(n_chan, fine),
+        fixed(features),
+        fixed(neighbours),
+        fixed(parent_index.reshape(1, -1)),
+        fixed(octant.reshape(1, -1)),
+        fixed(parent_dest.reshape(1, -1)),
+        fixed(conv_fine),
+        fixed(conv_down),
+        fixed(conv_coarse),
+        fixed(norm_gain.reshape(1, -1)),
+        fixed(table(n_chan, fine)),
     )
 
 

time: 29.4 us -> 26.3 us (0.89)
  Pallas kernels: 27.8 us -> 25.5 us
  local copies, waits for them, and re-layouts: 1.47 us -> 0.63 us
    pallas_call x1, Pallas kernels: 27.8 us -> 25.5 us  [body(): pl.pallas_call(functools.partial(fused_kernel, n_space, n_chan, bricks, s...]
    unnamed x1, local copies, waits for them, and re-layouts: 1.47 us -> 0.63 us
where the time goes in v2:
time: 26.3 us; the launch traced here: 26.1 us
  Pallas kernels  25.5 us (97%)
  local copies, waits for them, and re-layouts  0.63 us (2%)
    pallas_call x1, Pallas kernels, body(): pl.pallas_call(functools.partial(fused_kernel, n_space, n_chan, bricks, s...  25.5 us
    unnamed x1, local copies, waits for them, and re-layouts  0.63 us

profile of v2, /device:TPU:0, one launch (start us, length us, event | category | flops | bytes accessed | tf_op | source)
XLA Modules:
  0.0 26.1 jit_solution(1485323430979162142)
XLA Ops:
  0.0 25.5 %shard_map.100 = bf16[64,512]{1,0:T(8,128)(2,1)S(1)} custom-call(bf16[16,64,128]{2,1,0:T(8,128)(2,1)} %feat_hbm.1, s32[16,26]{1,0:T(8,128)} %nbr_hbm.1, s32[1,16]{1,0:T(1,128)} %bitcast.4, s32[1,16]{1,0:T(1,128)} %bitcast.5, s32[1,4]{1,0:T(1,128)} %bitcast.6, bf16[32,3456]{1,0:T(8,128)(2,1)} %wf_hbm.1, bf16[64,3456]{1,0:T(8,128)(2,1)} %wd_hbm.1, ...), custom_call_target="tpu_custom_call" | custom-call | tf_op jit(solution)/shard_map/pallas_call | solution.py:580
  25.5 0.6 %copy.12 = bf16[64,512]{1,0:T(8,128)(2,1)} copy(bf16[64,512]{1,0:T(8,128)(2,1)S(1)} %shard_map.100) | data formatting | bytes 131072

commit v3 on v2

--- a/solution.py
+++ b/solution.py
@@ -65,7 +65,7 @@
     feat_hbm, nbr_hbm, parent_hbm, octant_hbm, dest_hbm, wf_hbm, wd_hbm, wc_hbm, gain_hbm, perm_hbm,
     out,
     feat, nbr, wf, wt, gain, parent_in, octant_in, dest_in, meta, wd, wc, perm,
-    fh, mh, pbuf, part_h, g_buf, qbuf, c_buf, cp, cn, e_buf, hot_e, hot_o, pb, pw, ohd,
+    fh, mh, pbuf, part_h, g_buf, qbuf, c_buf, cp, cn, e_buf, hot_e, hot_o, acc, pb, pw, ohd,
     wsem, s1, r1, s2, r2, hs2, hr2, s3, r3, hs3, hr3, s4, r4, ws4, wr4,
 ):
     sp = lax.axis_index("space")
@@ -254,13 +254,11 @@
     for x in range(1, EDGE - 1):
         g_buf[me, x + 1] = jnp.maximum(total[x * line : (x + 1) * line], 0.0).astype(BF)
 
-    def finish(k, a, first, x, xq):
-        place(a, first, fh[k].reshape(bricks * FACE, fine), [xq])
+    def rest(a, xq):
         taps = wt[:, (a + 1) * 3 * reach : (a + 2) * 3 * reach]
-        rest = lax.dot_general(
+        return lax.dot_general(
             jnp.concatenate([cube(xq, b) for b in range(3)], axis=1), taps, NT, preferred_element_type=F32
         )
-        g_buf[me, x + 1] = jnp.maximum(part_h[k] + rest, 0.0).astype(BF)
 
     spans = ((2, EDGE - 2), (EDGE, 1), (1, 1))
 
@@ -281,22 +279,28 @@
     def _():
         dn_feat.wait_recv()
 
-    finish(1, 1, 2 * bricks, EDGE - 1, EDGE + 1)
-    for k, chan in enumerate(peers):
-        hid_copy(1, k, chan).start()
-
-    @pl.when(has_next)
-    def _():
-        for chan in range(n_chan):
-            rc(g_buf.at[me, EDGE], g_buf.at[me, 0], hs2.at[chan], hr2.at[me], sp + 1, chan).start()
-
     @pl.when(has_prev)
     def _():
         up_feat.wait_recv()
 
-    finish(0, -1, 0, 0, 0)
-    for k, chan in enumerate(peers):
-        hid_copy(2, k, chan).start()
+    place(1, 2 * bricks, fh[1].reshape(bricks * FACE, fine), [EDGE + 1])
+    place(-1, 0, fh[0].reshape(bricks * FACE, fine), [0])
+    g_buf[me, EDGE] = jnp.maximum(part_h[1] + rest(1, EDGE + 1), 0.0).astype(BF)
+    g_buf[me, 1] = jnp.maximum(part_h[0] + rest(-1, 0), 0.0).astype(BF)
+    for j in (1, 2):
+        for k, chan in enumerate(peers):
+            hid_copy(j, k, chan).start()
+
+    twin = me + 1 - 2 * lax.rem(me, 2)
+    spread_to = [lax.rem(c + 2 * j, n_chan) for j in range(n_chan // 2) for c in (me, twin)]
+
+    def hid_halo(k):
+        return rc(g_buf.at[me, EDGE], g_buf.at[me, 0], hs2.at[k], hr2.at[me], sp + 1, spread_to[k])
+
+    @pl.when(has_next)
+    def _():
+        for k in range(n_chan):
+            hid_halo(k).start()
 
     @pl.when(has_next)
     def _():
@@ -308,14 +312,15 @@
 
     lanes = meta.shape[1]
     lane_par = jnp.where(
-        iota((lanes, parents * cells), 1) // cells == iota((lanes, parents * cells), 0), 1.0, 0.0
+        iota((lanes, parents * cells), 1) % CLAYER // FACE == iota((lanes, parents * cells), 0), 1.0, 0.0
     )
 
     def dest_table(k):
         block = meta[...] if k == 1 else mh[k // 2]
         rel = jnp.dot(block.astype(F32), lane_par, preferred_element_type=F32)[1:2].astype(jnp.int32)
         slot = rel - (2 - k) * slots
-        target = slot * cells + iota((1, parents * cells), 1) % cells
+        at = iota((1, parents * cells), 1)
+        target = slot * cells + at // CLAYER * FACE + at % FACE
         ids = iota((slots * cells, parents * cells), 0)
         ohd[k] = one(ids == jnp.where((slot >= 0) & (slot < slots), target, -1))
 
@@ -357,19 +362,17 @@
     for load in loads[6:8]:
         load.wait()
 
-    for j in range(3):
-        hid_wait(j)
-
-    def unpack(first, number):
+    hid_wait(0)
+
+    full = EDGE * fine
+    tail = fine * (EDGE - 1)
+
+    def unpack(at):
         joined = jnp.concatenate(
-            [g_buf[s, first : first + number].reshape(number * line, group) for s in range(n_chan)], axis=1
+            [jnp.concatenate([g_buf[s, x + 1] for s in range(n_chan)], axis=1) for x in at], axis=0
         )
-        return pick(joined, perm[...]).astype(BF)
-
-    full = EDGE * fine
-    moved = unpack(1, EDGE)
-    for x in range(EDGE):
-        qbuf[x + 1, 1:LOW, :, fine : LOW * fine] = moved[x * line : (x + 1) * line].reshape(EDGE, bricks, full)
+        moved = pick(joined, perm[...]).astype(BF)
+        return [moved[i * line : (i + 1) * line] for i in range(len(at))]
 
     def hot_rows(a, c, n):
         col = iota((bricks, n), 1)
@@ -381,30 +384,27 @@
             rows.append(one(col == where))
         return jnp.concatenate(rows, axis=0)
 
-    tail = fine * (EDGE - 1)
-    edge_y = pick(
-        one(iota((bricks, bricks), 1) == loc_of(0, -1, 0) - bricks),
-        jnp.concatenate([moved[x * line + line - bricks : (x + 1) * line] for x in range(EDGE)], axis=1),
-    ).astype(BF)
-    edge_z = pick(
-        hot_rows(0, -1, line), jnp.concatenate([moved[x * line : (x + 1) * line, tail:] for x in range(EDGE)], axis=1)
-    ).astype(BF)
-    for x in range(EDGE):
-        qbuf[x + 1, 0, :, fine : LOW * fine] = edge_y[:, x * full : (x + 1) * full]
-        qbuf[x + 1, :, :, 0:fine] = edge_z[:, x * fine : (x + 1) * fine].reshape(LOW, bricks, fine)
-
-    @pl.when(has_prev)
-    def _():
-        for chan in range(n_chan):
-            rc(g_buf.at[chan, 0], g_buf.at[chan, 0], hs2.at[chan], hr2.at[chan], sp - 1, chan).wait_recv()
-
-    joint = jnp.concatenate([moved[tail // fine * line :], unpack(0, 1)], axis=0)
-    qbuf[0, :, :, fine : LOW * fine] = pick(hot_rows(-1, 0, 2 * line), joint).astype(BF).reshape(LOW, bricks, full)
-    qbuf[0, :, :, 0:fine] = pick(hot_rows(-1, -1, 2 * line), joint[:, tail:]).astype(BF).reshape(LOW, bricks, fine)
-
-    stacked = []
-    for qz in range(HALF):
-        for qx in range(HALF):
+    def lay_out(at):
+        moved = unpack(at)
+        edge_y = pick(
+            one(iota((bricks, bricks), 1) == loc_of(0, -1, 0) - bricks),
+            jnp.concatenate([m[line - bricks :] for m in moved], axis=1),
+        ).astype(BF)
+        edge_z = pick(hot_rows(0, -1, line), jnp.concatenate([m[:, tail:] for m in moved], axis=1)).astype(BF)
+        for i, x in enumerate(at):
+            qbuf[x + 1, 1:LOW, :, fine : LOW * fine] = moved[i].reshape(EDGE, bricks, full)
+            qbuf[x + 1, 0, :, fine : LOW * fine] = edge_y[:, i * full : (i + 1) * full]
+            qbuf[x + 1, :, :, 0:fine] = edge_z[:, i * fine : (i + 1) * fine].reshape(LOW, bricks, fine)
+        return moved
+
+    lay_out(list(range(1, EDGE - 1)))
+
+    for j in (1, 2):
+        hid_wait(j)
+
+    def down(qx):
+        stacked = []
+        for qz in range(HALF):
             for qy in range(HALF):
                 stacked.append(
                     jnp.concatenate(
@@ -416,23 +416,51 @@
                         axis=1,
                     )
                 )
-    pieces = lax.dot_general(jnp.concatenate(stacked, axis=0), wd[...], NT, preferred_element_type=F32)
-    pieces = jnp.maximum(pieces, 0.0)
-    part = 2 * side
-    c_buf[me] = jnp.concatenate([pieces[h * part : (h + 1) * part] for h in range(HALF)], axis=1).astype(BF)
-
+        pieces = lax.dot_general(jnp.concatenate(stacked, axis=0), wd[...], NT, preferred_element_type=F32)
+        pieces = jnp.maximum(pieces, 0.0)
+        c_buf[me, qx * side : (qx + 1) * side] = jnp.concatenate(
+            [pieces[h * side : (h + 1) * side] for h in range(HALF)], axis=1
+        ).astype(BF)
+
+    def part_copy(qx, k, chan):
+        ref = c_buf.at[me, pl.ds(qx * side, side)]
+        return rc(ref, ref, s3.at[qx, k], r3.at[qx, me], sp, chan)
+
+    def up_part(k):
+        return rc(c_buf.at[me, pl.ds(side, side)], cp.at[me], hs3.at[0, k], hr3.at[0, me], sp + 1, spread_to[k])
+
+    def dn_part(k):
+        return rc(c_buf.at[me, pl.ds(0, side)], cn.at[me], hs3.at[1, k], hr3.at[1, me], sp - 1, spread_to[k])
+
+    last = lay_out([0, EDGE - 1])[1]
+    down(1)
     for k, chan in enumerate(peers):
-        rc(c_buf.at[me], c_buf.at[me], s3.at[k], r3.at[me], sp, chan).start()
-
-    @pl.when(has_next)
-    def _():
-        for chan in range(n_chan):
-            rc(c_buf.at[me, pl.ds(side, side)], cp.at[me], hs3.at[0, chan], hr3.at[0, me], sp + 1, chan).start()
-
-    @pl.when(has_prev)
-    def _():
-        for chan in range(n_chan):
-            rc(c_buf.at[me, pl.ds(0, side)], cn.at[me], hs3.at[1, chan], hr3.at[1, me], sp - 1, chan).start()
+        part_copy(1, k, chan).start()
+
+    @pl.when(has_next)
+    def _():
+        for k in range(n_chan):
+            up_part(k).start()
+
+    @pl.when(has_prev)
+    def _():
+        for chan in range(n_chan):
+            rc(g_buf.at[chan, 0], g_buf.at[chan, 0], hs2.at[chan], hr2.at[chan], sp - 1, chan).wait_recv()
+
+    joint = jnp.concatenate(
+        [last, pick(jnp.concatenate([g_buf[s, 0] for s in range(n_chan)], axis=1), perm[...]).astype(BF)], axis=0
+    )
+    qbuf[0, :, :, fine : LOW * fine] = pick(hot_rows(-1, 0, 2 * line), joint).astype(BF).reshape(LOW, bricks, full)
+    qbuf[0, :, :, 0:fine] = pick(hot_rows(-1, -1, 2 * line), joint[:, tail:]).astype(BF).reshape(LOW, bricks, fine)
+    down(0)
+
+    for k, chan in enumerate(peers):
+        part_copy(0, k, chan).start()
+
+    @pl.when(has_prev)
+    def _():
+        for k in range(n_chan):
+            dn_part(k).start()
 
     for load in loads[8:]:
         load.wait()
@@ -441,9 +469,11 @@
         jnp.where(iota((own, own), 0) == iota((own, own), 1), gain[...], 0.0), axis=1, keepdims=True
     )
 
-    for k in range(1, n_chan):
-        src = lax.rem(me + k, n_chan)
-        rc(c_buf.at[src], c_buf.at[src], s3.at[0], r3.at[src], sp, src).wait_recv()
+    for qx in range(HALF):
+        for k in range(1, n_chan):
+            src = lax.rem(me + k, n_chan)
+            ref = c_buf.at[src, pl.ds(qx * side, side)]
+            rc(ref, ref, s3.at[qx, 0], r3.at[qx, src], sp, src).wait_recv()
 
     def all_channels(buf):
         return jnp.concatenate(
@@ -454,19 +484,11 @@
             axis=0,
         )
 
-    def coarse_taps(a):
+    def coarse_taps(a, at):
         blocks = []
         for bc in range(TAPS2):
-            blocks.append(
-                jnp.concatenate(
-                    [
-                        e_buf[x + a, bc * CLAYER + g * FACE : bc * CLAYER + (g + 1) * FACE, :]
-                        for g in range(parents)
-                        for x in range(CX)
-                    ],
-                    axis=0,
-                )
-            )
+            rows = slice(bc * CLAYER, (bc + 1) * CLAYER)
+            blocks.append(jnp.concatenate([e_buf[x + a, rows] for x in at], axis=0))
         span = TAPS2 * coarse
         taps = wc[:, a * span : (a + 1) * span]
         return lax.dot_general(taps, jnp.concatenate(blocks, axis=1), NT, preferred_element_type=F32)
@@ -474,7 +496,12 @@
     inside = all_channels(c_buf)
     for x in range(CX):
         e_buf[x + 1] = pick(hot_e[x], inside).astype(BF)
-    total = coarse_taps(1)
+    total = coarse_taps(1, range(CX))
+    low = coarse_taps(0, range(1, CX))
+    high = coarse_taps(2, range(CX - 1))
+    acc[...] = total
+    acc[:, CLAYER:] += low
+    acc[:, : (CX - 1) * CLAYER] += high
 
     @pl.when(has_prev)
     def _():
@@ -488,7 +515,13 @@
 
     e_buf[0] = pick(hot_o[0], all_channels(cp)).astype(BF)
     e_buf[CX + 1] = pick(hot_o[1], all_channels(cn)).astype(BF)
-    total = total + coarse_taps(0) + coarse_taps(2)
+    low = coarse_taps(0, [0])
+    high = coarse_taps(2, [CX - 1])
+    total = acc[...]
+    edge = (CX - 1) * CLAYER
+    total = jnp.concatenate(
+        [total[:, :CLAYER] + low, total[:, CLAYER:edge], total[:, edge:] + high], axis=1
+    )
     rounded = total.astype(BF)
     pb[1] = rounded
     values = rounded.astype(F32)
@@ -538,7 +571,8 @@
     for k, chan in enumerate(peers):
         for j in range(3):
             hid_copy(j, k, chan).wait_send()
-        rc(c_buf.at[me], c_buf.at[me], s3.at[k], r3.at[me], sp, chan).wait_send()
+        for qx in range(HALF):
+            part_copy(qx, k, chan).wait_send()
         rc(pw.at[1, me], pw.at[1, me], ws4.at[1, k], wr4.at[1, me], sp, chan).wait_send()
 
     @pl.when(has_next)
@@ -547,8 +581,8 @@
         up_feat.wait_send()
         rc(pb.at[1], pb.at[0], s4.at[0], r4.at[0], sp + 1, me).wait_send()
         for chan in range(n_chan):
-            rc(g_buf.at[me, EDGE], g_buf.at[me, 0], hs2.at[chan], hr2.at[me], sp + 1, chan).wait_send()
-            rc(c_buf.at[me, pl.ds(side, side)], cp.at[me], hs3.at[0, chan], hr3.at[0, me], sp + 1, chan).wait_send()
+            hid_halo(chan).wait_send()
+            up_part(chan).wait_send()
             rc(pw.at[1, me], pw.at[0, me], ws4.at[0, chan], wr4.at[0, me], sp + 1, chan).wait_send()
 
     @pl.when(has_prev)
@@ -557,7 +591,7 @@
         dn_feat.wait_send()
         rc(pb.at[1], pb.at[2], s4.at[1], r4.at[1], sp - 1, me).wait_send()
         for chan in range(n_chan):
-            rc(c_buf.at[me, pl.ds(0, side)], cn.at[me], hs3.at[1, chan], hr3.at[1, me], sp - 1, chan).wait_send()
+            dn_part(chan).wait_send()
             rc(pw.at[1, me], pw.at[2, me], ws4.at[2, chan], wr4.at[2, me], sp - 1, chan).wait_send()
 
 
@@ -607,6 +641,7 @@
             pltpu.VMEM((CX + 2, TAPS2 * CLAYER, coarse), BF),
             pltpu.VMEM((CX, TAPS2 * CLAYER, HALF**3 * bricks), BF),
             pltpu.VMEM((2, TAPS2 * CLAYER, HALF**2 * bricks), BF),
+            pltpu.VMEM((own, parents * cells), F32),
             pltpu.VMEM((3, own, parents * cells), BF),
             pltpu.VMEM((3, n_chan, 1, parents * cells), F32),
             pltpu.VMEM((3, slots * cells, parents * cells), BF),
@@ -617,8 +652,8 @@
             dma((3, n_chan)),
             dma((n_chan,)),
             dma((n_chan,)),
-            dma((n_chan - 1,)),
-            dma((n_chan,)),
+            dma((HALF, n_chan - 1)),
+            dma((HALF, n_chan)),
             dma((2, n_chan)),
             dma((2, n_chan)),
             dma((2,)),

time: 26.3 us -> 24.8 us (0.943)
  Pallas kernels: 25.5 us -> 24 us
    pallas_call x1, Pallas kernels: 25.5 us -> 24 us  [body(): pl.pallas_call(functools.partial(fused_kernel, n_space, n_chan, bricks, s...]
where the time goes in v3:
time: 24.8 us; the launch traced here: 24.7 us
  Pallas kernels  24 us (97%)
  local copies, waits for them, and re-layouts  0.63 us (3%)
    pallas_call x1, Pallas kernels, body(): pl.pallas_call(functools.partial(fused_kernel, n_space, n_chan, bricks, s...  24 us
    unnamed x1, local copies, waits for them, and re-layouts  0.63 us

profile of v3, /device:TPU:0, one launch (start us, length us, event | category | flops | bytes accessed | tf_op | source)
XLA Modules:
  0.0 24.7 jit_solution(4758139069979234416)
XLA Ops:
  0.0 24.0 %shard_map.100 = bf16[64,512]{1,0:T(8,128)(2,1)S(1)} custom-call(bf16[16,64,128]{2,1,0:T(8,128)(2,1)} %feat_hbm.1, s32[16,26]{1,0:T(8,128)} %nbr_hbm.1, s32[1,16]{1,0:T(1,128)} %bitcast.4, s32[1,16]{1,0:T(1,128)} %bitcast.5, s32[1,4]{1,0:T(1,128)} %bitcast.6, bf16[32,3456]{1,0:T(8,128)(2,1)} %wf_hbm.1, bf16[64,3456]{1,0:T(8,128)(2,1)} %wd_hbm.1, ...), custom_call_target="tpu_custom_call" | custom-call | tf_op jit(solution)/shard_map/pallas_call | solution.py:614
  24.0 0.6 %copy.12 = bf16[64,512]{1,0:T(8,128)(2,1)} copy(bf16[64,512]{1,0:T(8,128)(2,1)S(1)} %shard_map.100) | data formatting | bytes 131072

commit v4 on v3

--- a/solution.py
+++ b/solution.py
@@ -65,7 +65,7 @@
     feat_hbm, nbr_hbm, parent_hbm, octant_hbm, dest_hbm, wf_hbm, wd_hbm, wc_hbm, gain_hbm, perm_hbm,
     out,
     feat, nbr, wf, wt, gain, parent_in, octant_in, dest_in, meta, wd, wc, perm,
-    fh, mh, pbuf, part_h, g_buf, qbuf, c_buf, cp, cn, e_buf, hot_e, hot_o, acc, pb, pw, ohd,
+    fh, mh, pbuf, part_h, g_buf, qbuf, c_buf, cp, cn, e_buf, hot_e, acc, pair, single, kept, pb, pw, ohd,
     wsem, s1, r1, s2, r2, hs2, hr2, s3, r3, hs3, hr3, s4, r4, ws4, wr4,
 ):
     sp = lax.axis_index("space")
@@ -284,12 +284,14 @@
         up_feat.wait_recv()
 
     place(1, 2 * bricks, fh[1].reshape(bricks * FACE, fine), [EDGE + 1])
+    g_buf[me, EDGE] = jnp.maximum(part_h[1] + rest(1, EDGE + 1), 0.0).astype(BF)
+    for k, chan in enumerate(peers):
+        hid_copy(1, k, chan).start()
+
     place(-1, 0, fh[0].reshape(bricks * FACE, fine), [0])
-    g_buf[me, EDGE] = jnp.maximum(part_h[1] + rest(1, EDGE + 1), 0.0).astype(BF)
     g_buf[me, 1] = jnp.maximum(part_h[0] + rest(-1, 0), 0.0).astype(BF)
-    for j in (1, 2):
-        for k, chan in enumerate(peers):
-            hid_copy(j, k, chan).start()
+    for k, chan in enumerate(peers):
+        hid_copy(2, k, chan).start()
 
     twin = me + 1 - 2 * lax.rem(me, 2)
     spread_to = [lax.rem(c + 2 * j, n_chan) for j in range(n_chan // 2) for c in (me, twin)]
@@ -320,41 +322,31 @@
         rel = jnp.dot(block.astype(F32), lane_par, preferred_element_type=F32)[1:2].astype(jnp.int32)
         slot = rel - (2 - k) * slots
         at = iota((1, parents * cells), 1)
-        target = slot * cells + at // CLAYER * FACE + at % FACE
+        row = at % (HALF * CLAYER)
+        target = slot * cells + (2 * (row // CLAYER) + at // (HALF * CLAYER)) * FACE + at % FACE
         ids = iota((slots * cells, parents * cells), 0)
         ohd[k] = one(ids == jnp.where((slot >= 0) & (slot < slots), target, -1))
 
-    n_own = HALF**3 * bricks
-    spread = jnp.where(iota((lanes, n_own), 1) % bricks == iota((lanes, n_own), 0), 1.0, 0.0)
-
-    def codes(block, n):
-        code = jnp.dot(block.astype(F32), spread[:, 0:n], preferred_element_type=F32)[0:1].astype(jnp.int32)
-        return code % 2, code // 2 % SLAB_Y, code // (2 * SLAB_Y)
-
-    def wants(n, bc):
-        at = iota((CLAYER, n), 0)
-        par, yz = at // FACE, at % FACE
+    n_hot = HALF * HALF * bricks
+    spread = jnp.where(iota((lanes, n_hot), 1) % bricks == iota((lanes, n_hot), 0), 1.0, 0.0)
+
+    def key_of(block):
+        code = jnp.dot(block.astype(F32), spread, preferred_element_type=F32)[0:1].astype(jnp.int32)
+        sub = iota((1, n_hot), 1) // bricks
+        y = 2 * (code // 2 % SLAB_Y) + sub % HALF
+        z = 2 * (code // (2 * SLAB_Y)) + sub // HALF
+        return code % 2, y * CZ + z
+
+    keys = [(mh[0], 1), (meta[...], 0), (meta[...], 1), (mh[1], 0)]
+    keys = [jnp.where(x_bit == want, key, -1) for (x_bit, key), want in ((key_of(m), w) for m, w in keys)]
+    at = iota((CLAYER, n_hot), 0)
+    par, yz = at // FACE, at % FACE
+    for bc in range(TAPS2):
         y = par // (SLAB_Z // 2) * EDGE + yz // EDGE + bc // 3 - 1
         z = par % (SLAB_Z // 2) * EDGE + yz % EDGE + bc % 3 - 1
-        return jnp.where((y >= 0) & (y < CY) & (z >= 0) & (z < CZ), y * CZ + z, FAR)
-
-    x_bit, y_at, z_at = codes(meta[...], n_own)
-    sub = iota((1, n_own), 1) // bricks
-    key = (2 * y_at + sub % HALF) * CZ + 2 * z_at + sub // (HALF * HALF)
-    layer = 2 * x_bit + sub // HALF % HALF
-    for bc in range(TAPS2):
-        want = wants(n_own, bc)
-        for x in range(CX):
-            hot_e[x, bc * CLAYER : (bc + 1) * CLAYER] = one(want == jnp.where(layer == x, key, -1))
-
-    n_out = HALF * HALF * bricks
-    for k in range(2):
-        x_bit, y_at, z_at = codes(mh[k], n_out)
-        sub = iota((1, n_out), 1) // bricks
-        key = (2 * y_at + sub % HALF) * CZ + 2 * z_at + sub // HALF
-        key = jnp.where(x_bit == 1 - k, key, -1)
-        for bc in range(TAPS2):
-            hot_o[k, bc * CLAYER : (bc + 1) * CLAYER] = one(wants(n_out, bc) == key)
+        want = jnp.where((y >= 0) & (y < CY) & (z >= 0) & (z < CZ), y * CZ + z, FAR)
+        for k in range(4):
+            hot_e[k, bc * CLAYER : (bc + 1) * CLAYER] = one(want == keys[k])
 
     for k in range(3):
         dest_table(k)
@@ -469,104 +461,125 @@
         jnp.where(iota((own, own), 0) == iota((own, own), 1), gain[...], 0.0), axis=1, keepdims=True
     )
 
-    for qx in range(HALF):
+    def part_wait(qx):
         for k in range(1, n_chan):
             src = lax.rem(me + k, n_chan)
             ref = c_buf.at[src, pl.ds(qx * side, side)]
             rc(ref, ref, s3.at[qx, 0], r3.at[qx, src], sp, src).wait_recv()
 
-    def all_channels(buf):
+    def all_channels(blocks):
         return jnp.concatenate(
             [
-                jnp.concatenate([buf[s][:, h * own_d : (h + 1) * own_d] for s in range(n_chan)], axis=1)
+                jnp.concatenate([block[:, h * own_d : (h + 1) * own_d] for block in blocks], axis=1)
                 for h in range(HALF)
             ],
             axis=0,
         )
 
-    def coarse_taps(a, at):
-        blocks = []
-        for bc in range(TAPS2):
-            rows = slice(bc * CLAYER, (bc + 1) * CLAYER)
-            blocks.append(jnp.concatenate([e_buf[x + a, rows] for x in at], axis=0))
-        span = TAPS2 * coarse
-        taps = wc[:, a * span : (a + 1) * span]
-        return lax.dot_general(taps, jnp.concatenate(blocks, axis=1), NT, preferred_element_type=F32)
-
-    inside = all_channels(c_buf)
-    for x in range(CX):
-        e_buf[x + 1] = pick(hot_e[x], inside).astype(BF)
-    total = coarse_taps(1, range(CX))
-    low = coarse_taps(0, range(1, CX))
-    high = coarse_taps(2, range(CX - 1))
-    acc[...] = total
-    acc[:, CLAYER:] += low
-    acc[:, : (CX - 1) * CLAYER] += high
-
+    def fill(qx):
+        inside = all_channels([c_buf[s, qx * side : (qx + 1) * side] for s in range(n_chan)])
+        for x_bit in range(2):
+            e_buf[2 * x_bit + qx + 1] = pick(hot_e[1 + x_bit], inside).astype(BF)
+
+    span = TAPS2 * coarse
+
+    def blocks(layers):
+        return [
+            jnp.concatenate([e_buf[x, bc * CLAYER : (bc + 1) * CLAYER] for x in layers], axis=0)
+            for bc in range(TAPS2)
+        ]
+
+    def tap(a, layers):
+        return lax.dot_general(
+            wc[:, a * span : (a + 1) * span], jnp.concatenate(blocks(layers), axis=1), NT, preferred_element_type=F32
+        )
+
+    def pb_copy(side_k, h):
+        step = 1 - 2 * side_k
+        return rc(pb.at[1, h], pb.at[2 * side_k, h], s4.at[side_k, h], r4.at[side_k, h], sp + step, me)
+
+    def settle(h, total):
+        rounded = total.astype(BF)
+        pb[1, h] = rounded
+        values = rounded.astype(F32)
+        pw[1, me, h] = jnp.sum(values * values, axis=0, keepdims=True)
+
+        @pl.when(has_next)
+        def _():
+            pb_copy(0, h).start()
+
+        @pl.when(has_prev)
+        def _():
+            pb_copy(1, h).start()
+
+    part_wait(1)
+    fill(1)
+    acc[1] = tap(1, [2, 4])
+    pair[0] = tap(2, [2, 4])
+    single[0] = tap(0, [2])
     @pl.when(has_prev)
     def _():
         for chan in range(n_chan):
             rc(cp.at[chan], cp.at[chan], hs3.at[0, chan], hr3.at[0, chan], sp - 1, chan).wait_recv()
 
+    e_buf[0] = pick(hot_e[0], all_channels([cp[s] for s in range(n_chan)])).astype(BF)
+    acc[0] = pair[0] + jnp.concatenate([tap(0, [0]), single[0]], axis=1)
+    part_wait(0)
+    fill(0)
+    acc[0] += tap(1, [1, 3])
+    pair[1] = acc[1] + tap(0, [1, 3])
+    single[1] = tap(2, [3])
+    settle(0, acc[0])
     @pl.when(has_next)
     def _():
         for chan in range(n_chan):
             rc(cn.at[chan], cn.at[chan], hs3.at[1, chan], hr3.at[1, chan], sp + 1, chan).wait_recv()
 
-    e_buf[0] = pick(hot_o[0], all_channels(cp)).astype(BF)
-    e_buf[CX + 1] = pick(hot_o[1], all_channels(cn)).astype(BF)
-    low = coarse_taps(0, [0])
-    high = coarse_taps(2, [CX - 1])
-    total = acc[...]
-    edge = (CX - 1) * CLAYER
-    total = jnp.concatenate(
-        [total[:, :CLAYER] + low, total[:, CLAYER:edge], total[:, edge:] + high], axis=1
-    )
-    rounded = total.astype(BF)
-    pb[1] = rounded
-    values = rounded.astype(F32)
-    pw[1, me] = jnp.sum(values * values, axis=0, keepdims=True)
+    e_buf[CX + 1] = pick(hot_e[3], all_channels([cn[s] for s in range(n_chan)])).astype(BF)
+    settle(1, pair[1] + jnp.concatenate([single[1], tap(2, [5])], axis=1))
 
     for k, chan in enumerate(peers):
         rc(pw.at[1, me], pw.at[1, me], ws4.at[1, k], wr4.at[1, me], sp, chan).start()
 
     @pl.when(has_next)
     def _():
-        rc(pb.at[1], pb.at[0], s4.at[0], r4.at[0], sp + 1, me).start()
-        for chan in range(n_chan):
-            rc(pw.at[1, me], pw.at[0, me], ws4.at[0, chan], wr4.at[0, me], sp + 1, chan).start()
-
-    @pl.when(has_prev)
-    def _():
-        rc(pb.at[1], pb.at[2], s4.at[1], r4.at[1], sp - 1, me).start()
-        for chan in range(n_chan):
-            rc(pw.at[1, me], pw.at[2, me], ws4.at[2, chan], wr4.at[2, me], sp - 1, chan).start()
+        for k in range(n_chan):
+            rc(pw.at[1, me], pw.at[0, me], ws4.at[0, k], wr4.at[0, me], sp + 1, spread_to[k]).start()
+
+    @pl.when(has_prev)
+    def _():
+        for k in range(n_chan):
+            rc(pw.at[1, me], pw.at[2, me], ws4.at[2, k], wr4.at[2, me], sp - 1, spread_to[k]).start()
 
     def normed(k):
-        power = pw[k, 0]
-        for s in range(1, n_chan):
-            power = power + pw[k, s]
-        scaled = pb[k].astype(F32) * lax.rsqrt(power / coarse + epsilon) * gain_col
-        return lax.dot_general(scaled.astype(BF), ohd[k], NT, preferred_element_type=F32)
+        halves = []
+        for h in range(HALF):
+            power = pw[k, 0, h]
+            for s in range(1, n_chan):
+                power = power + pw[k, s, h]
+            halves.append((pb[k, h].astype(F32) * lax.rsqrt(power / coarse + epsilon) * gain_col).astype(BF))
+        return lax.dot_general(jnp.concatenate(halves, axis=1), ohd[k], NT, preferred_element_type=F32)
 
     for k in range(1, n_chan):
         src = lax.rem(me + k, n_chan)
         rc(pw.at[1, src], pw.at[1, src], ws4.at[1, 0], wr4.at[1, src], sp, src).wait_recv()
-    result = normed(1)
-
-    @pl.when(has_prev)
-    def _():
-        rc(pb.at[0], pb.at[0], s4.at[0], r4.at[0], sp - 1, me).wait_recv()
+    kept[...] = normed(1)
+
+    @pl.when(has_prev)
+    def _():
+        for h in range(HALF):
+            pb_copy(0, h).wait_recv()
         for chan in range(n_chan):
             rc(pw.at[0, chan], pw.at[0, chan], ws4.at[0, chan], wr4.at[0, chan], sp - 1, chan).wait_recv()
 
     @pl.when(has_next)
     def _():
-        rc(pb.at[2], pb.at[2], s4.at[1], r4.at[1], sp + 1, me).wait_recv()
+        for h in range(HALF):
+            pb_copy(1, h).wait_recv()
         for chan in range(n_chan):
             rc(pw.at[2, chan], pw.at[2, chan], ws4.at[2, chan], wr4.at[2, chan], sp + 1, chan).wait_recv()
 
-    out[...] = (result + normed(0) + normed(2)).astype(BF)
+    out[...] = (kept[...] + normed(0) + normed(2)).astype(BF)
 
     for k, chan in enumerate(peers):
         for j in range(3):
@@ -579,20 +592,22 @@
     def _():
         up_meta.wait_send()
         up_feat.wait_send()
-        rc(pb.at[1], pb.at[0], s4.at[0], r4.at[0], sp + 1, me).wait_send()
+        for h in range(HALF):
+            pb_copy(0, h).wait_send()
         for chan in range(n_chan):
             hid_halo(chan).wait_send()
             up_part(chan).wait_send()
-            rc(pw.at[1, me], pw.at[0, me], ws4.at[0, chan], wr4.at[0, me], sp + 1, chan).wait_send()
+            rc(pw.at[1, me], pw.at[0, me], ws4.at[0, chan], wr4.at[0, me], sp + 1, spread_to[chan]).wait_send()
 
     @pl.when(has_prev)
     def _():
         dn_meta.wait_send()
         dn_feat.wait_send()
-        rc(pb.at[1], pb.at[2], s4.at[1], r4.at[1], sp - 1, me).wait_send()
+        for h in range(HALF):
+            pb_copy(1, h).wait_send()
         for chan in range(n_chan):
             dn_part(chan).wait_send()
-            rc(pw.at[1, me], pw.at[2, me], ws4.at[2, chan], wr4.at[2, me], sp - 1, chan).wait_send()
+            rc(pw.at[1, me], pw.at[2, me], ws4.at[2, chan], wr4.at[2, me], sp - 1, spread_to[chan]).wait_send()
 
 
 def body(n_space, n_chan, features, neighbours, parent_index, octant, parent_dest, conv_fine, conv_down, conv_coarse, norm_gain):
@@ -639,11 +654,13 @@
             pltpu.VMEM((n_chan, HALF * bricks, HALF * own_d), BF),
             pltpu.VMEM((n_chan, HALF * bricks, HALF * own_d), BF),
             pltpu.VMEM((CX + 2, TAPS2 * CLAYER, coarse), BF),
-            pltpu.VMEM((CX, TAPS2 * CLAYER, HALF**3 * bricks), BF),
-            pltpu.VMEM((2, TAPS2 * CLAYER, HALF**2 * bricks), BF),
-            pltpu.VMEM((own, parents * cells), F32),
-            pltpu.VMEM((3, own, parents * cells), BF),
-            pltpu.VMEM((3, n_chan, 1, parents * cells), F32),
+            pltpu.VMEM((4, TAPS2 * CLAYER, HALF**2 * bricks), BF),
+            pltpu.VMEM((HALF, own, HALF * CLAYER), F32),
+            pltpu.VMEM((HALF, own, HALF * CLAYER), F32),
+            pltpu.VMEM((HALF, own, CLAYER), F32),
+            pltpu.VMEM((own, slots * cells), F32),
+            pltpu.VMEM((3, HALF, own, HALF * CLAYER), BF),
+            pltpu.VMEM((3, n_chan, HALF, 1, HALF * CLAYER), F32),
             pltpu.VMEM((3, slots * cells, parents * cells), BF),
             dma((10,)),
             dma((2, 2)),
@@ -656,8 +673,8 @@
             dma((HALF, n_chan)),
             dma((2, n_chan)),
             dma((2, n_chan)),
-            dma((2,)),
-            dma((2,)),
+            dma((2, HALF)),
+            dma((2, HALF)),
             dma((3, n_chan)),
             dma((3, n_chan)),
         ],

time: 24.8 us -> 24.2 us (0.976)
  Pallas kernels: 24 us -> 23.4 us
    pallas_call x1, Pallas kernels: 24 us -> 23.4 us  [body(): pl.pallas_call(functools.partial(fused_kernel, n_space, n_chan, bricks, s...]
where the time goes in v4:
time: 24.2 us; the launch traced here: 24.1 us
  Pallas kernels  23.4 us (97%)
  local copies, waits for them, and re-layouts  0.63 us (3%)
    pallas_call x1, Pallas kernels, body(): pl.pallas_call(functools.partial(fused_kernel, n_space, n_chan, bricks, s...  23.4 us
    unnamed x1, local copies, waits for them, and re-layouts  0.63 us

profile of v4, /device:TPU:0, one launch (start us, length us, event | category | flops | bytes accessed | tf_op | source)
XLA Modules:
  0.0 24.1 jit_solution(6725300892264854750)
XLA Ops:
  0.0 23.4 %shard_map.100 = bf16[64,512]{1,0:T(8,128)(2,1)S(1)} custom-call(bf16[16,64,128]{2,1,0:T(8,128)(2,1)} %feat_hbm.1, s32[16,26]{1,0:T(8,128)} %nbr_hbm.1, s32[1,16]{1,0:T(1,128)} %bitcast.4, s32[1,16]{1,0:T(1,128)} %bitcast.5, s32[1,4]{1,0:T(1,128)} %bitcast.6, bf16[32,3456]{1,0:T(8,128)(2,1)} %wf_hbm.1, bf16[64,3456]{1,0:T(8,128)(2,1)} %wd_hbm.1, ...), custom_call_target="tpu_custom_call" | custom-call | tf_op jit(solution)/shard_map/pallas_call | solution.py:629
  23.4 0.6 %copy.12 = bf16[64,512]{1,0:T(8,128)(2,1)} copy(bf16[64,512]{1,0:T(8,128)(2,1)S(1)} %shard_map.100) | data formatting | bytes 131072

commit v5 on v4

--- a/solution.py
+++ b/solution.py
@@ -65,7 +65,7 @@
     feat_hbm, nbr_hbm, parent_hbm, octant_hbm, dest_hbm, wf_hbm, wd_hbm, wc_hbm, gain_hbm, perm_hbm,
     out,
     feat, nbr, wf, wt, gain, parent_in, octant_in, dest_in, meta, wd, wc, perm,
-    fh, mh, pbuf, part_h, g_buf, qbuf, c_buf, cp, cn, e_buf, hot_e, acc, pair, single, kept, pb, pw, ohd,
+    fh, mh, pbuf, part_h, g_buf, qbuf, c_buf, cp, cn, e_buf, hot_e, acc, pair, single, kept, kept_row, base, pb, pw, ohd,
     wsem, s1, r1, s2, r2, hs2, hr2, s3, r3, hs3, hr3, s4, r4, ws4, wr4,
 ):
     sp = lax.axis_index("space")
@@ -288,21 +288,21 @@
     for k, chan in enumerate(peers):
         hid_copy(1, k, chan).start()
 
+    twin = me + 1 - 2 * lax.rem(me, 2)
+    spread_to = [lax.rem(c + 2 * j, n_chan) for j in range(n_chan // 2) for c in (me, twin)]
+
+    def hid_halo(k):
+        return rc(g_buf.at[me, EDGE], g_buf.at[me, 0], hs2.at[k], hr2.at[me], sp + 1, spread_to[k])
+
+    @pl.when(has_next)
+    def _():
+        for k in range(n_chan):
+            hid_halo(k).start()
+
     place(-1, 0, fh[0].reshape(bricks * FACE, fine), [0])
     g_buf[me, 1] = jnp.maximum(part_h[0] + rest(-1, 0), 0.0).astype(BF)
     for k, chan in enumerate(peers):
         hid_copy(2, k, chan).start()
-
-    twin = me + 1 - 2 * lax.rem(me, 2)
-    spread_to = [lax.rem(c + 2 * j, n_chan) for j in range(n_chan // 2) for c in (me, twin)]
-
-    def hid_halo(k):
-        return rc(g_buf.at[me, EDGE], g_buf.at[me, 0], hs2.at[k], hr2.at[me], sp + 1, spread_to[k])
-
-    @pl.when(has_next)
-    def _():
-        for k in range(n_chan):
-            hid_halo(k).start()
 
     @pl.when(has_next)
     def _():
@@ -361,7 +361,7 @@
 
     def unpack(at):
         joined = jnp.concatenate(
-            [jnp.concatenate([g_buf[s, x + 1] for s in range(n_chan)], axis=1) for x in at], axis=0
+            [jnp.concatenate([g_buf[s, x] for s in range(n_chan)], axis=1) for x in at], axis=0
         )
         moved = pick(joined, perm[...]).astype(BF)
         return [moved[i * line : (i + 1) * line] for i in range(len(at))]
@@ -376,8 +376,7 @@
             rows.append(one(col == where))
         return jnp.concatenate(rows, axis=0)
 
-    def lay_out(at):
-        moved = unpack(at)
+    def lay_out(at, moved):
         edge_y = pick(
             one(iota((bricks, bricks), 1) == loc_of(0, -1, 0) - bricks),
             jnp.concatenate([m[line - bricks :] for m in moved], axis=1),
@@ -387,14 +386,11 @@
             qbuf[x + 1, 1:LOW, :, fine : LOW * fine] = moved[i].reshape(EDGE, bricks, full)
             qbuf[x + 1, 0, :, fine : LOW * fine] = edge_y[:, i * full : (i + 1) * full]
             qbuf[x + 1, :, :, 0:fine] = edge_z[:, i * fine : (i + 1) * fine].reshape(LOW, bricks, fine)
-        return moved
-
-    lay_out(list(range(1, EDGE - 1)))
-
-    for j in (1, 2):
-        hid_wait(j)
-
-    def down(qx):
+    lay_out(list(range(1, EDGE - 1)), unpack(list(range(2, EDGE))))
+
+    hid_wait(1)
+
+    def down_taps(qx, taps):
         stacked = []
         for qz in range(HALF):
             for qy in range(HALF):
@@ -402,13 +398,17 @@
                     jnp.concatenate(
                         [
                             qbuf[2 * qx + a, 2 * qy + b, :, 2 * qz * fine : (2 * qz + 3) * fine]
-                            for a in range(3)
+                            for a in taps
                             for b in range(3)
                         ],
                         axis=1,
                     )
                 )
-        pieces = lax.dot_general(jnp.concatenate(stacked, axis=0), wd[...], NT, preferred_element_type=F32)
+        rows = jnp.concatenate(stacked, axis=0)
+        at = taps[0] * TAPS2 * fine
+        return lax.dot_general(rows, wd[:, at : at + rows.shape[1]], NT, preferred_element_type=F32)
+
+    def down(qx, pieces):
         pieces = jnp.maximum(pieces, 0.0)
         c_buf[me, qx * side : (qx + 1) * side] = jnp.concatenate(
             [pieces[h * side : (h + 1) * side] for h in range(HALF)], axis=1
@@ -424,8 +424,10 @@
     def dn_part(k):
         return rc(c_buf.at[me, pl.ds(0, side)], cn.at[me], hs3.at[1, k], hr3.at[1, me], sp - 1, spread_to[k])
 
-    last = lay_out([0, EDGE - 1])[1]
-    down(1)
+    last = unpack([EDGE])
+    lay_out([EDGE - 1], last)
+    kept_row[...] = last[0]
+    down(1, down_taps(1, range(3)))
     for k, chan in enumerate(peers):
         part_copy(1, k, chan).start()
 
@@ -434,17 +436,18 @@
         for k in range(n_chan):
             up_part(k).start()
 
+    hid_wait(2)
+    lay_out([0], unpack([1]))
+    base[...] = down_taps(0, range(1, 3))
     @pl.when(has_prev)
     def _():
         for chan in range(n_chan):
             rc(g_buf.at[chan, 0], g_buf.at[chan, 0], hs2.at[chan], hr2.at[chan], sp - 1, chan).wait_recv()
 
-    joint = jnp.concatenate(
-        [last, pick(jnp.concatenate([g_buf[s, 0] for s in range(n_chan)], axis=1), perm[...]).astype(BF)], axis=0
-    )
+    joint = jnp.concatenate([kept_row[...], unpack([0])[0]], axis=0)
     qbuf[0, :, :, fine : LOW * fine] = pick(hot_rows(-1, 0, 2 * line), joint).astype(BF).reshape(LOW, bricks, full)
     qbuf[0, :, :, 0:fine] = pick(hot_rows(-1, -1, 2 * line), joint[:, tail:]).astype(BF).reshape(LOW, bricks, fine)
-    down(0)
+    down(0, base[...] + down_taps(0, range(1)))
 
     for k, chan in enumerate(peers):
         part_copy(0, k, chan).start()
@@ -659,6 +662,8 @@
             pltpu.VMEM((HALF, own, HALF * CLAYER), F32),
             pltpu.VMEM((HALF, own, CLAYER), F32),
             pltpu.VMEM((own, slots * cells), F32),
+            pltpu.VMEM((EDGE * bricks, EDGE * fine), BF),
+            pltpu.VMEM((HALF * HALF * bricks, own_d), F32),
             pltpu.VMEM((3, HALF, own, HALF * CLAYER), BF),
             pltpu.VMEM((3, n_chan, HALF, 1, HALF * CLAYER), F32),
             pltpu.VMEM((3, slots * cells, parents * cells), BF),

time: 24.2 us -> 24.2 us (level)
  no operation moved by 1% of the time
where the time goes in v5:
time: 24.2 us; the launch traced here: 24.1 us
  Pallas kernels  23.4 us (97%)
  local copies, waits for them, and re-layouts  0.63 us (3%)
    pallas_call x1, Pallas kernels, body(): pl.pallas_call(functools.partial(fused_kernel, n_space, n_chan, bricks, s...  23.4 us
    unnamed x1, local copies, waits for them, and re-layouts  0.63 us

profile of v5, /device:TPU:0, one launch (start us, length us, event | category | flops | bytes accessed | tf_op | source)
XLA Modules:
  0.0 24.1 jit_solution(4368594533367137508)
XLA Ops:
  0.0 23.4 %shard_map.100 = bf16[64,512]{1,0:T(8,128)(2,1)S(1)} custom-call(bf16[16,64,128]{2,1,0:T(8,128)(2,1)} %feat_hbm.1, s32[16,26]{1,0:T(8,128)} %nbr_hbm.1, s32[1,16]{1,0:T(1,128)} %bitcast.4, s32[1,16]{1,0:T(1,128)} %bitcast.5, s32[1,4]{1,0:T(1,128)} %bitcast.6, bf16[32,3456]{1,0:T(8,128)(2,1)} %wf_hbm.1, bf16[64,3456]{1,0:T(8,128)(2,1)} %wd_hbm.1, ...), custom_call_target="tpu_custom_call" | custom-call | tf_op jit(solution)/shard_map/pallas_call | solution.py:632
  23.4 0.6 %copy.12 = bf16[64,512]{1,0:T(8,128)(2,1)} copy(bf16[64,512]{1,0:T(8,128)(2,1)S(1)} %shard_map.100) | data formatting | bytes 131072
